TPU v7x, 32 devices: a whole 2x2x4 slice. The times are simulated.
32 devices in a mesh: groups: 2 (over y), seq: 4 (over z), rows: 4 (over x, core).
Axes of the slice: x: 2, y: 2, z: 4, core: 2. Of those that a mesh axis runs over, the one named last changes fastest.
Arguments:
- layer_inputs: bfloat16 [8, 128, 4096], P(('groups', 'rows'), 'seq'), parts along dimension 0, may hold values from -6 to 6
- out_grads: bfloat16 [8, 128, 4096], P(('groups', 'rows'), 'seq'), parts along dimension 0, may hold values from -6 to 6
- input_proj: bfloat16 [4096, 128], P('seq'), may hold values from -0.09375 to 0.09375
- grad_proj: bfloat16 [4096, 128], P('seq'), may hold values from -0.09375 to 0.09375
- query_lengths: int32 [8], P(('groups', 'rows')), parts along dimension 0, may hold values from 1 to 128, as said below
- train_store: float32 [2048, 16384], P(('groups', 'rows'), 'seq'), parts along dimension 0, may hold values from -0.00390625 to 0.00390625
Outputs:
- influence: float32 [8, 1024], P(('groups', 'seq'), 'rows'), parts along dimension 0
There are 2 independent parts, one for each index of `groups`. A program takes and returns all parts, laid end to end along the dimension named above; an argument that names none is the same for every part. Nothing has to cross between parts.
Inputs may be any that keep to these rules, and one draw needn't show every extreme that they name: `query_lengths`: some query of every draw has all 128 tokens.
All inputs are finite; a program needn't handle non-finite values.
Results may differ from a plain program's by a relative error of at most 0.0003.
Values may be sent and summed in bfloat16 or wider, within the bound.
No kernel may reach another device: no remote copies, remote signals or barrier semaphores. Data moves between devices by JAX's collectives and lax.ppermute only.
A program may use at most 64 MiB of HBM per device.

v0:
```python
import functools

import jax
import jax.numpy as jnp
from jax import lax
from jax.experimental import pallas as pl
from jax.experimental.pallas import tpu as pltpu
from jax.sharding import PartitionSpec as P


LANES = 128
VMEM = pl.BlockSpec(memory_space=pltpu.VMEM)
HBM = pl.BlockSpec(memory_space=pltpu.HBM)
SMEM = pl.BlockSpec(memory_space=pltpu.SMEM)


ROUTES = {
    "tokens": ((3, 2, 0, 1), (2, 3, 1, 0), (1, 0, 3, 2)),
    "scores": ((1, 2, 3, 0), (2, 3, 0, 1), (3, 0, 1, 2)),
}


def routes(stage, n):
    if n == 4 and stage in ROUTES:
        return ROUTES[stage]
    if n & (n - 1) == 0:
        order = list(range(n - 1, 0, -1))
        if stage == "tokens":
            order = order[:1] + order[:0:-1]
        return [tuple(d ^ k for d in range(n)) for k in order]
    return [tuple((d + k) % n for d in range(n)) for k in range(1, n)]


def inverse(route):
    return tuple(route.index(d) for d in range(len(route)))


def entry(route, d):
    if all(t == a ^ route[0] for a, t in enumerate(route)):
        return d ^ route[0]
    at = route[0]
    for a, t in enumerate(route[1:], 1):
        at = jnp.where(d == a, t, at)
    return at


def exchange(arrays, axis, n, stage):
    got = []
    for i, route in enumerate(routes(stage, n)):
        got.append(lax.ppermute(arrays[i], axis, list(enumerate(route))))
    return got


def in_place(array):
    return pltpu.with_memory_space_constraint(array, pltpu.HBM)


def call(kernel, outs, in_specs, scratch=(), mib=16):
    return pl.pallas_call(
        kernel,
        out_shape=[jax.ShapeDtypeStruct(*o) for o in outs],
        in_specs=list(in_specs),
        out_specs=[VMEM] * len(outs),
        scratch_shapes=list(scratch),
        compiler_params=pltpu.CompilerParams(vmem_limit_bytes=mib << 20),
    )


def slice_copies(sources, at, width, out, sem):
    at = pl.multiple_of(at * width, width)
    return [
        pltpu.make_async_copy(src.at[0, :, pl.ds(at, width)], out.at[j], sem.at[j])
        for j, src in enumerate(sources)
    ]


def run_all(copies):
    for c in copies:
        c.start()
    for c in copies:
        c.wait()


def pack_kernel(x, g, *rest, n, width):
    outs, sem = rest[:-1], rest[-1]
    s = lax.axis_index("seq")
    copies = []
    for i, route in enumerate(routes("tokens", n)):
        copies += slice_copies((x, g), entry(route, s), width, outs[i], sem.at[i])
    run_all(copies)


def fetch_kernel(after, x, g, *rest, width):
    count = (len(rest) - 3) // 2
    sources, outs, own = rest[:count], rest[count : 2 * count], rest[2 * count]
    own_sem, sem = rest[2 * count + 1 :]
    copies = slice_copies((x, g), lax.axis_index("seq"), width, own, own_sem)
    for j, (src, out) in enumerate(zip(sources, outs)):
        copies.append(pltpu.make_async_copy(src, out, sem.at[j]))
    run_all(copies)


def feature_kernel(*refs, n, n_tok, block):
    toks, w_in, w_out = refs[:n], refs[n], refs[n + 1]
    outs, rows = refs[n + 2 : 2 * n + 2], refs[2 * n + 2]
    s = lax.axis_index("seq")
    source = [s] + [entry(inverse(route), s) for route in routes("tokens", n)]
    to = [s] + [entry(route, s) for route in routes("features", n)]
    total = n * n_tok
    for k in range(n):
        at = pl.multiple_of(source[k] * n_tok, n_tok)
        for j in range(2):
            rows[j, pl.ds(at, n_tok), :] = toks[k][j]
    first = jnp.dot(rows[0], w_in[...], preferred_element_type=jnp.float32)
    second = jnp.dot(rows[1], w_out[...], preferred_element_type=jnp.float32)
    turned = refs[2 * n + 3]
    for c in range(total // LANES):
        turned[c] = second[c * LANES : (c + 1) * LANES].T
    for k in range(n):
        at = pl.multiple_of(to[k] * block, block)
        outs[k][:total] = first
        for c in range(total // LANES):
            outs[k][total + c * block : total + (c + 1) * block] = turned[c, pl.ds(at, block), :]


def gradient_kernel(length, *refs, n, total, block):
    parts, out = refs[:n], refs[n]
    whole = parts[0][...]
    for part in parts[1:]:
        whole = whole + part[...]
    acc = None
    for c in range(total // LANES):
        feat_out = whole[total + c * block : total + (c + 1) * block]
        at = c * LANES + lax.broadcasted_iota(jnp.int32, feat_out.shape, 1)
        feat_out = jnp.where(at < length[0], feat_out, 0.0)
        prod = jnp.dot(
            feat_out,
            whole[c * LANES : (c + 1) * LANES],
            precision=lax.Precision.HIGHEST,
            preferred_element_type=jnp.float32,
        )
        acc = prod if acc is None else acc + prod
    out[...] = acc


def lane_scores(grads, store, block, step, sums):
    m = len(grads)

    def rows_step(t, carry):
        at = pl.multiple_of(t * step, step)
        acc = [jnp.zeros((step, LANES), jnp.float32) for _ in range(m)]
        for i in range(block):
            tile = store[pl.ds(at, step), i * LANES : (i + 1) * LANES]
            for k in range(m):
                acc[k] = acc[k] + tile * grads[k][i : i + 1, :]
        for k in range(m):
            sums[k, pl.ds(at, step), :] = acc[k]
        return carry

    lax.fori_loop(0, store.shape[0] // step, rows_step, 0)
    return [jnp.sum(sums[k].T, axis=0, keepdims=True) for k in range(m)]


def early_kernel(*refs, block, step):
    grads, (store, out, sums) = refs[:-3], refs[-3:]
    for k, row in enumerate(lane_scores(grads, store, block, step, sums)):
        out[k] = row


def late_kernel(early, *refs, n, m, first, late, block, step):
    grads, store = refs[: len(late)], refs[len(late)]
    outs, (rows, sums) = refs[len(late) + 1 : -2], refs[-2:]
    s, r = lax.axis_index("seq"), lax.axis_index("rows")
    query = [r] + [entry(inverse(route), r) for route in routes("gradient", m)]
    for j, k in enumerate(first):
        rows[query[k]] = early[j]
    for k, row in zip(late, lane_scores(grads, store, block, step, sums)):
        rows[query[k]] = row
    for k, target in enumerate([s] + [entry(route, s) for route in routes("scores", n)]):
        outs[k][...] = rows[target]


def body(layer_inputs, out_grads, input_proj, grad_proj, query_lengths, train_store):
    n, m = lax.axis_size("seq"), lax.axis_size("rows")
    _, n_tok, _ = layer_inputs.shape
    total = n * n_tok
    part, feats = input_proj.shape
    n_rows, coords = train_store.shape
    block = coords // feats
    f32 = jnp.float32

    tokens_in = in_place(layer_inputs), in_place(out_grads)
    slices = ((2, n_tok, part), layer_inputs.dtype)
    packed = call(
        functools.partial(pack_kernel, n=n, width=part),
        [slices] * (n - 1),
        [HBM, HBM],
        [pltpu.SemaphoreType.DMA((n - 1, 2))],
    )(*tokens_in)
    held = (input_proj, grad_proj, train_store)
    input_proj, grad_proj, train_store, own = call(
        functools.partial(fetch_kernel, width=part),
        [(a.shape, a.dtype) for a in held] + [slices],
        [VMEM] + [HBM] * 5,
        [pltpu.SemaphoreType.DMA((2,)), pltpu.SemaphoreType.DMA((3,))],
    )(packed[0], *tokens_in, *map(in_place, held))
    tokens = [own] + exchange(packed, "seq", n, "tokens")

    height = total + total * block // LANES
    partial = call(
        functools.partial(feature_kernel, n=n, n_tok=n_tok, block=block),
        [((height, LANES), f32)] * n,
        [VMEM] * (n + 2),
        [pltpu.VMEM((2, total, part), layer_inputs.dtype), pltpu.VMEM((total // LANES, feats, LANES), f32)],
    )(*tokens, input_proj, grad_proj)
    parts = [partial[0]] + exchange(partial[1:], "seq", n, "features")

    (grad,) = call(
        functools.partial(gradient_kernel, n=n, total=total, block=block),
        [((block, LANES), f32)],
        [SMEM] + [VMEM] * n,
    )(query_lengths, *parts)
    grads = [grad] + exchange([grad] * (m - 1), "rows", m, "gradient")

    first, late = (0, m - 1), tuple(range(1, m - 1))
    (early,) = call(
        functools.partial(early_kernel, block=block, step=128),
        [((len(first), 1, n_rows), f32)],
        [VMEM] * (len(first) + 1),
        [pltpu.VMEM((len(first), n_rows, LANES), f32)],
    )(*(grads[k] for k in first), train_store)
    step = 128 if len(late) <= 4 else 8
    scores = call(
        functools.partial(late_kernel, n=n, m=m, first=first, late=late, block=block, step=step),
        [((1, n_rows), f32)] * n,
        [VMEM] * (len(late) + 2),
        [pltpu.VMEM((m, 1, n_rows), f32), pltpu.VMEM((len(late), n_rows, LANES), f32)],
    )(early, *(grads[k] for k in late), train_store)
    out = scores[0]
    for other in exchange(scores[1:], "seq", n, "scores"):
        out = out + other
    return out


def solution(mesh):
    in_specs = (
        P(("groups", "rows"), "seq", None),
        P(("groups", "rows"), "seq", None),
        P("seq", None),
        P("seq", None),
        P(("groups", "rows")),
        P(("groups", "rows"), "seq"),
    )
    out_specs = P(("groups", "seq"), "rows")

    return jax.shard_map(body, mesh=mesh, in_specs=in_specs, out_specs=out_specs, check_vma=False)
```

profile of v0, /device:TPU:0, one launch (start us, length us, event | category | flops | bytes accessed | tf_op | source)
XLA Modules:
  0.0 41.7 jit_solution(12750374411125881427)
XLA Ops:
  0.0 1.1 %shard_map.64 = (bf16[2,32,1024]{2,1,0:T(8,128)(2,1)S(1)}, bf16[2,32,1024]{2,1,0:T(8,128)(2,1)S(1)}, bf16[2,32,1024]{2,1,0:T(8,128)(2,1)S(1)}) custom-call(bf16[1,32,4096]{2,1,0:T(8,128)(2,1)} %x.3, bf16[1,32,4096]{2,1,0:T(8,128)(2,1)} %g.3), custom_call_target="tpu_custom_call" | custom-call | tf_op jit(solution)/shard_map/pallas_call | solution.py:194
  1.1 5.1 %collective-permute-start = (bf16[2,32,1024]{2,1,0:T(8,128)(2,1)S(1)}, bf16[2,32,1024]{2,1,0:T(8,128)(2,1)S(1)}, u32[]{:S(2)}, u32[]{:S(2)}) collective-permute-start(bf16[2,32,1024]{2,1,0:T(8,128)(2,1)S(1)} %get-tuple-element.20.after), channel_id=1, source_target_pairs={{0,12},{4,8},{8,0},{12,4},{1,13},{5,9},{9,1},{13,5},{2,14},{6,10},... | collective-permute-start | bytes 393224 | tf_op jit(solution)/shard_map/ppermute | solution.py:50
  6.2 0.0 collective-permute-start.1
  6.2 0.9 %collective-permute-start.2 = (bf16[2,32,1024]{2,1,0:T(8,128)(2,1)S(1)}, bf16[2,32,1024]{2,1,0:T(8,128)(2,1)S(1)}, u32[]{:S(2)}, u32[]{:S(2)}) collective-permute-start(bf16[2,32,1024]{2,1,0:T(8,128)(2,1)S(1)} %get-tuple-element.23), channel_id=1, source_target_pairs={{0,4},{4,0},{8,12},{12,8},{1,5},{5,1},{9,13},{13,9},{2,6},{6,2},{1... | collective-permute-start | bytes 393224 | tf_op jit(solution)/shard_map/ppermute | solution.py:50
  7.1 2.4 %shard_map.65 = (bf16[1024,128]{1,0:T(8,128)(2,1)S(1)}, bf16[1024,128]{1,0:T(8,128)(2,1)S(1)}, f32[256,4096]{1,0:T(8,128)S(1)}, bf16[2,32,1024]{2,1,0:T(8,128)(2,1)S(1)}) custom-call(bf16[2,32,1024]{2,1,0:T(8,128)(2,1)S(1)} %get-tuple-element.20.after, bf16[1,32,4096]{2,1,0:T(8,128)(2,1)} %x.3, bf16[1,32,4096]{2,1,0:T(8,128)(2,1)} %g.3, ...), custom_call_target="tpu_custom_call" | custom-call | tf_op jit(solution)/shard_map/pallas_call | solution.py:201
  9.5 5.7 %collective-permute-done.refs_1_ = bf16[2,32,1024]{2,1,0:T(8,128)(2,1)S(1)} collective-permute-done((bf16[2,32,1024]{2,1,0:T(8,128)(2,1)S(1)}, bf16[2,32,1024]{2,1,0:T(8,128)(2,1)S(1)}, u32[]{:S(2)}, u32[]{:S(2)}) %collective-permute-start) | collective-permute-done | bytes 131104 | tf_op jit(solution)/shard_map/ppermute | solution.py:50
  15.2 0.0 collective-permute-done.1.refs_2_
  15.2 0.4 %collective-permute-done.2.refs_3_ = bf16[2,32,1024]{2,1,0:T(8,128)(2,1)S(1)} collective-permute-done((bf16[2,32,1024]{2,1,0:T(8,128)(2,1)S(1)}, bf16[2,32,1024]{2,1,0:T(8,128)(2,1)S(1)}, u32[]{:S(2)}, u32[]{:S(2)}) %collective-permute-start.2) | collective-permute-done | bytes 131104 | tf_op jit(solution)/shard_map/ppermute | solution.py:50
  15.6 0.4 shard_map.66
  16.0 4.2 %collective-permute-start.3 = (f32[160,128]{1,0:T(8,128)S(1)}, f32[160,128]{1,0:T(8,128)S(1)}, u32[]{:S(2)}, u32[]{:S(2)}) collective-permute-start(f32[160,128]{1,0:T(8,128)S(1)} %get-tuple-element.27), channel_id=1, source_target_pairs={{0,12},{4,8},{8,4},{12,0},{1,13},{5,9},{9,5},{13,1},{2,14},{6,10},... | collective-permute-start | bytes 245768 | tf_op jit(solution)/shard_map/ppermute | solution.py:50
  20.2 0.0 collective-permute-start.4
  20.2 0.6 %collective-permute-start.5 = (f32[160,128]{1,0:T(8,128)S(1)}, f32[160,128]{1,0:T(8,128)S(1)}, u32[]{:S(2)}, u32[]{:S(2)}) collective-permute-start(f32[160,128]{1,0:T(8,128)S(1)} %get-tuple-element.29), channel_id=1, source_target_pairs={{0,4},{4,0},{8,12},{12,8},{1,5},{5,1},{9,13},{13,9},{2,6},{6,2},{1... | collective-permute-start | bytes 245768 | tf_op jit(solution)/shard_map/ppermute | solution.py:50
  21.5 1.4 %collective-permute-done.3.refs_1_ = f32[160,128]{1,0:T(8,128)S(1)} collective-permute-done((f32[160,128]{1,0:T(8,128)S(1)}, f32[160,128]{1,0:T(8,128)S(1)}, u32[]{:S(2)}, u32[]{:S(2)}) %collective-permute-start.3) | collective-permute-done | bytes 81952 | tf_op jit(solution)/shard_map/ppermute | solution.py:50
  22.9 3.6 %collective-permute-done.4.refs_2_ = f32[160,128]{1,0:T(8,128)S(1)} collective-permute-done((f32[160,128]{1,0:T(8,128)S(1)}, f32[160,128]{1,0:T(8,128)S(1)}, u32[]{:S(2)}, u32[]{:S(2)}) %collective-permute-start.4) | collective-permute-done | bytes 81952 | tf_op jit(solution)/shard_map/ppermute | solution.py:50
  26.5 0.0 collective-permute-done.5.refs_3_
  26.5 0.2 shard_map.67.refs_0_
  26.7 0.0 collective-permute-start.6
  26.7 1.5 %collective-permute-start.7 = (f32[32,128]{1,0:T(8,128)S(1)}, f32[32,128]{1,0:T(8,128)S(1)}, u32[]{:S(2)}, u32[]{:S(2)}) collective-permute-start(f32[32,128]{1,0:T(8,128)S(1)} %shard_map.67.refs_0_), channel_id=1, source_target_pairs={{0,3},{1,2},{2,1},{3,0},{4,7},{5,6},{6,5},{7,4},{8,11},{9,10},{10,... | collective-permute-start | bytes 49160 | tf_op jit(solution)/shard_map/ppermute | solution.py:50
  28.1 0.7 %collective-permute-start.8 = (f32[32,128]{1,0:T(8,128)S(1)}, f32[32,128]{1,0:T(8,128)S(1)}, u32[]{:S(2)}, u32[]{:S(2)}) collective-permute-start(f32[32,128]{1,0:T(8,128)S(1)} %shard_map.67.refs_0_), channel_id=1, source_target_pairs={{0,2},{1,3},{2,0},{3,1},{4,6},{5,7},{6,4},{7,5},{8,10},{9,11},{10,... | collective-permute-start | bytes 49160 | tf_op jit(solution)/shard_map/ppermute | solution.py:50
  28.8 0.0 collective-permute-done.6.refs_1_
  28.8 0.7 %shard_map.68.early = f32[2,1,256]{2,1,0:T(1,128)S(1)} custom-call(f32[32,128]{1,0:T(8,128)S(1)} %shard_map.67.refs_0_, f32[32,128]{1,0:T(8,128)S(1)} %collective-permute-done.6.refs_1_, f32[256,4096]{1,0:T(8,128)S(1)} %get-tuple-element.30.refs_2_), custom_call_target="tpu_custom_call" | custom-call | tf_op jit(solution)/shard_map/pallas_call | solution.py:226
  29.6 0.3 collective-permute-done.7.refs_0_
  29.9 2.0 %collective-permute-done.8.refs_1_ = f32[32,128]{1,0:T(8,128)S(1)} collective-permute-done((f32[32,128]{1,0:T(8,128)S(1)}, f32[32,128]{1,0:T(8,128)S(1)}, u32[]{:S(2)}, u32[]{:S(2)}) %collective-permute-start.8) | collective-permute-done | bytes 16416 | tf_op jit(solution)/shard_map/ppermute | solution.py:50
  31.9 0.7 %shard_map.69 = (f32[1,256]{1,0:T(1,128)S(1)}, f32[1,256]{1,0:T(1,128)S(1)}, f32[1,256]{1,0:T(1,128)S(1)}, f32[1,256]{1,0:T(1,128)S(1)}) custom-call(f32[2,1,256]{2,1,0:T(1,128)S(1)} %shard_map.68.early, f32[32,128]{1,0:T(8,128)S(1)} %collective-permute-done.7.refs_0_, f32[32,128]{1,0:T(8,128)S(1)} %collective-permute-done.8.refs_1_, ...), custom_call_target="tpu_custom_call" | custom-call | tf_op jit(solution)/shard_map/pallas_call | solution.py:233
  32.6 1.3 %collective-permute-start.10 = (f32[1,256]{1,0:T(1,128)S(1)}, f32[1,256]{1,0:T(1,128)S(1)}, u32[]{:S(2)}, u32[]{:S(2)}) collective-permute-start(f32[1,256]{1,0:T(1,128)S(1)} %get-tuple-element.33), channel_id=1, source_target_pairs={{0,8},{4,12},{8,0},{12,4},{1,9},{5,13},{9,1},{13,5},{2,10},{6,14},... | collective-permute-start | bytes 3080 | tf_op jit(solution)/shard_map/ppermute | solution.py:50
  33.9 1.9 %collective-permute-start.11 = (f32[1,256]{1,0:T(1,128)S(1)}, f32[1,256]{1,0:T(1,128)S(1)}, u32[]{:S(2)}, u32[]{:S(2)}) collective-permute-start(f32[1,256]{1,0:T(1,128)S(1)} %get-tuple-element.34), channel_id=1, source_target_pairs={{0,12},{4,0},{8,4},{12,8},{1,13},{5,1},{9,5},{13,9},{2,14},{6,2},{... | collective-permute-start | bytes 3080 | tf_op jit(solution)/shard_map/ppermute | solution.py:50
  35.8 0.2 collective-permute-start.9
  35.9 1.2 %collective-permute-done.10 = f32[1,256]{1,0:T(1,128)S(1)} collective-permute-done((f32[1,256]{1,0:T(1,128)S(1)}, f32[1,256]{1,0:T(1,128)S(1)}, u32[]{:S(2)}, u32[]{:S(2)}) %collective-permute-start.10) | collective-permute-done | bytes 1056 | tf_op jit(solution)/shard_map/ppermute | solution.py:50
  37.1 0.3 collective-permute-done.11
  37.5 3.7 %collective-permute-done.9 = f32[1,256]{1,0:T(1,128)S(1)} collective-permute-done((f32[1,256]{1,0:T(1,128)S(1)}, f32[1,256]{1,0:T(1,128)S(1)}, u32[]{:S(2)}, u32[]{:S(2)}) %collective-permute-start.9) | collective-permute-done | bytes 1056 | tf_op jit(solution)/shard_map/ppermute | solution.py:50
  41.1 0.6 %add_add_fusion = f32[1,256]{1,0:T(1,128)} fusion(f32[1,256]{1,0:T(1,128)S(1)} %collective-permute-done.11, f32[1,256]{1,0:T(1,128)S(1)} %collective-permute-done.10, f32[1,256]{1,0:T(1,128)S(1)} %get-tuple-element.31, f32[1,256]{1,0:T(1,128)S(1)} %collective-permute-done.9), kind=kLoop, calls=%fused_computation | loop fusion | flops 768 | bytes 5120 | tf_op jit(solution)/shard_map/add | solution.py:241
Async XLA Ops:
  1.1 14.1 %collective-permute-start = (bf16[2,32,1024]{2,1,0:T(8,128)(2,1)S(1)}, bf16[2,32,1024]{2,1,0:T(8,128)(2,1)S(1)}, u32[]{:S(2)}, u32[]{:S(2)}) collective-permute-start(bf16[2,32,1024]{2,1,0:T(8,128)(2,1)S(1)} %get-tuple-element.20.after), channel_id=1, source_target_pairs={{0,12},{4,8},{8,0},{12,4},{1,13},{5,9},{9,1},{13,5},{2,14},{6,10},... | collective-permute-start | bytes 393224 | tf_op jit(solution)/shard_map/ppermute | solution.py:50
  6.2 9.0 %collective-permute-start.1 = (bf16[2,32,1024]{2,1,0:T(8,128)(2,1)S(1)}, bf16[2,32,1024]{2,1,0:T(8,128)(2,1)S(1)}, u32[]{:S(2)}, u32[]{:S(2)}) collective-permute-start(bf16[2,32,1024]{2,1,0:T(8,128)(2,1)S(1)} %get-tuple-element.22), channel_id=1, source_target_pairs={{0,8},{4,12},{8,4},{12,0},{1,9},{5,13},{9,5},{13,1},{2,10},{6,14},... | collective-permute-start | bytes 393224 | tf_op jit(solution)/shard_map/ppermute | solution.py:50
  6.2 9.4 %collective-permute-start.2 = (bf16[2,32,1024]{2,1,0:T(8,128)(2,1)S(1)}, bf16[2,32,1024]{2,1,0:T(8,128)(2,1)S(1)}, u32[]{:S(2)}, u32[]{:S(2)}) collective-permute-start(bf16[2,32,1024]{2,1,0:T(8,128)(2,1)S(1)} %get-tuple-element.23), channel_id=1, source_target_pairs={{0,4},{4,0},{8,12},{12,8},{1,5},{5,1},{9,13},{13,9},{2,6},{6,2},{1... | collective-permute-start | bytes 393224 | tf_op jit(solution)/shard_map/ppermute | solution.py:50
  16.0 6.9 %collective-permute-start.3 = (f32[160,128]{1,0:T(8,128)S(1)}, f32[160,128]{1,0:T(8,128)S(1)}, u32[]{:S(2)}, u32[]{:S(2)}) collective-permute-start(f32[160,128]{1,0:T(8,128)S(1)} %get-tuple-element.27), channel_id=1, source_target_pairs={{0,12},{4,8},{8,4},{12,0},{1,13},{5,9},{9,5},{13,1},{2,14},{6,10},... | collective-permute-start | bytes 245768 | tf_op jit(solution)/shard_map/ppermute | solution.py:50
  20.2 6.3 %collective-permute-start.4 = (f32[160,128]{1,0:T(8,128)S(1)}, f32[160,128]{1,0:T(8,128)S(1)}, u32[]{:S(2)}, u32[]{:S(2)}) collective-permute-start(f32[160,128]{1,0:T(8,128)S(1)} %get-tuple-element.28), channel_id=1, source_target_pairs={{0,8},{4,12},{8,0},{12,4},{1,9},{5,13},{9,1},{13,5},{2,10},{6,14},... | collective-permute-start | bytes 245768 | tf_op jit(solution)/shard_map/ppermute | solution.py:50
  20.2 6.3 %collective-permute-start.5 = (f32[160,128]{1,0:T(8,128)S(1)}, f32[160,128]{1,0:T(8,128)S(1)}, u32[]{:S(2)}, u32[]{:S(2)}) collective-permute-start(f32[160,128]{1,0:T(8,128)S(1)} %get-tuple-element.29), channel_id=1, source_target_pairs={{0,4},{4,0},{8,12},{12,8},{1,5},{5,1},{9,13},{13,9},{2,6},{6,2},{1... | collective-permute-start | bytes 245768 | tf_op jit(solution)/shard_map/ppermute | solution.py:50
  26.7 2.2 %collective-permute-start.6 = (f32[32,128]{1,0:T(8,128)S(1)}, f32[32,128]{1,0:T(8,128)S(1)}, u32[]{:S(2)}, u32[]{:S(2)}) collective-permute-start(f32[32,128]{1,0:T(8,128)S(1)} %shard_map.67.refs_0_), channel_id=1, source_target_pairs={{0,1},{1,0},{2,3},{3,2},{4,5},{5,4},{6,7},{7,6},{8,9},{9,8},{10,11... | collective-permute-start | bytes 49160 | tf_op jit(solution)/shard_map/ppermute | solution.py:50
  26.7 3.2 %collective-permute-start.7 = (f32[32,128]{1,0:T(8,128)S(1)}, f32[32,128]{1,0:T(8,128)S(1)}, u32[]{:S(2)}, u32[]{:S(2)}) collective-permute-start(f32[32,128]{1,0:T(8,128)S(1)} %shard_map.67.refs_0_), channel_id=1, source_target_pairs={{0,3},{1,2},{2,1},{3,0},{4,7},{5,6},{6,5},{7,4},{8,11},{9,10},{10,... | collective-permute-start | bytes 49160 | tf_op jit(solution)/shard_map/ppermute | solution.py:50
  28.1 3.7 %collective-permute-start.8 = (f32[32,128]{1,0:T(8,128)S(1)}, f32[32,128]{1,0:T(8,128)S(1)}, u32[]{:S(2)}, u32[]{:S(2)}) collective-permute-start(f32[32,128]{1,0:T(8,128)S(1)} %shard_map.67.refs_0_), channel_id=1, source_target_pairs={{0,2},{1,3},{2,0},{3,1},{4,6},{5,7},{6,4},{7,5},{8,10},{9,11},{10,... | collective-permute-start | bytes 49160 | tf_op jit(solution)/shard_map/ppermute | solution.py:50
  32.6 4.5 %collective-permute-start.10 = (f32[1,256]{1,0:T(1,128)S(1)}, f32[1,256]{1,0:T(1,128)S(1)}, u32[]{:S(2)}, u32[]{:S(2)}) collective-permute-start(f32[1,256]{1,0:T(1,128)S(1)} %get-tuple-element.33), channel_id=1, source_target_pairs={{0,8},{4,12},{8,0},{12,4},{1,9},{5,13},{9,1},{13,5},{2,10},{6,14},... | collective-permute-start | bytes 3080 | tf_op jit(solution)/shard_map/ppermute | solution.py:50
  33.9 3.6 %collective-permute-start.11 = (f32[1,256]{1,0:T(1,128)S(1)}, f32[1,256]{1,0:T(1,128)S(1)}, u32[]{:S(2)}, u32[]{:S(2)}) collective-permute-start(f32[1,256]{1,0:T(1,128)S(1)} %get-tuple-element.34), channel_id=1, source_target_pairs={{0,12},{4,0},{8,4},{12,8},{1,13},{5,1},{9,5},{13,9},{2,14},{6,2},{... | collective-permute-start | bytes 3080 | tf_op jit(solution)/shard_map/ppermute | solution.py:50
  35.8 5.4 %collective-permute-start.9 = (f32[1,256]{1,0:T(1,128)S(1)}, f32[1,256]{1,0:T(1,128)S(1)}, u32[]{:S(2)}, u32[]{:S(2)}) collective-permute-start(f32[1,256]{1,0:T(1,128)S(1)} %get-tuple-element.32), channel_id=1, source_target_pairs={{0,4},{4,8},{8,12},{12,0},{1,5},{5,9},{9,13},{13,1},{2,6},{6,10},{... | collective-permute-start | bytes 3080 | tf_op jit(solution)/shard_map/ppermute | solution.py:50
where the time goes:
time: 41.9 us; the launch traced here: 41.7 us
  waiting for transfers between devices  18.6 us (44%)
  starting transfers between devices  16.3 us (39%)
  Pallas kernels  5.47 us (13%)
  between operations  0.7 us (2%)
  other arithmetic  0.57 us (1%)
    ppermute x12, waiting for transfers between devices, exchange(): got.append(lax.ppermute(arrays[i], axis, list(enumerate(route))))  18.6 us
    ppermute x12, starting transfers between devices, exchange(): got.append(lax.ppermute(arrays[i], axis, list(enumerate(route))))  16.3 us
    pallas_call x1, Pallas kernels, body(): call(functools.partial(fetch_kernel, width=part), [(a.shape, a.dtype) for...  2.4 us
    pallas_call x1, Pallas kernels, body(): call(functools.partial(pack_kernel, n=n, width=part), [slices] * (n - 1),...  1.05 us
  transfers between devices with their start and end apart: 12, of which 9 were waited for; matrix products, arithmetic and copies ran while one was open for 0% of the time, Pallas kernels for 8%

commit v1 on v0

--- a/solution.py
+++ b/solution.py
@@ -15,6 +15,7 @@
 
 
 ROUTES = {
+    "features": ((2, 3, 0, 1), (1, 2, 3, 0), (3, 0, 1, 2)),
     "tokens": ((3, 2, 0, 1), (2, 3, 1, 0), (1, 0, 3, 2)),
     "scores": ((1, 2, 3, 0), (2, 3, 0, 1), (3, 0, 1, 2)),
 }
@@ -161,19 +162,29 @@
     return [jnp.sum(sums[k].T, axis=0, keepdims=True) for k in range(m)]
 
 
-def early_kernel(*refs, block, step):
-    grads, (store, out, sums) = refs[:-3], refs[-3:]
+def step_for(group, n_rows):
+    step = 256 // len(group) // 8 * 8
+    while n_rows % step:
+        step -= 8
+    return step
+
+
+def early_kernel(*refs, count, block, step):
+    grads, (store, out, sums) = refs[:count], refs[-3:]
     for k, row in enumerate(lane_scores(grads, store, block, step, sums)):
         out[k] = row
 
 
-def late_kernel(early, *refs, n, m, first, late, block, step):
+def late_kernel(*refs, n, m, groups, block, step):
+    ready, late = groups[:-1], groups[-1]
+    done, refs = refs[: len(ready)], refs[len(ready) :]
     grads, store = refs[: len(late)], refs[len(late)]
     outs, (rows, sums) = refs[len(late) + 1 : -2], refs[-2:]
     s, r = lax.axis_index("seq"), lax.axis_index("rows")
     query = [r] + [entry(inverse(route), r) for route in routes("gradient", m)]
-    for j, k in enumerate(first):
-        rows[query[k]] = early[j]
+    for group, part in zip(ready, done):
+        for j, k in enumerate(group):
+            rows[query[k]] = part[j]
     for k, row in zip(late, lane_scores(grads, store, block, step, sums)):
         rows[query[k]] = row
     for k, target in enumerate([s] + [entry(route, s) for route in routes("scores", n)]):
@@ -222,20 +233,23 @@
     )(query_lengths, *parts)
     grads = [grad] + exchange([grad] * (m - 1), "rows", m, "gradient")
 
-    first, late = (0, m - 1), tuple(range(1, m - 1))
-    (early,) = call(
-        functools.partial(early_kernel, block=block, step=128),
-        [((len(first), 1, n_rows), f32)],
-        [VMEM] * (len(first) + 1),
-        [pltpu.VMEM((len(first), n_rows, LANES), f32)],
-    )(*(grads[k] for k in first), train_store)
-    step = 128 if len(late) <= 4 else 8
+    groups = ((0, m - 1), tuple(range(1, m // 2)), tuple(range(m // 2, m - 1)))
+    ready = []
+    for group in groups[:-1]:
+        ready += call(
+            functools.partial(early_kernel, count=len(group), block=block, step=step_for(group, n_rows)),
+            [((len(group), 1, n_rows), f32)],
+            [VMEM] * (len(group) + 1 + len(ready)),
+            [pltpu.VMEM((len(group), n_rows, LANES), f32)],
+        )(*(grads[k] for k in group), *ready, train_store)
+    late = groups[-1]
+    step = step_for(late, n_rows)
     scores = call(
-        functools.partial(late_kernel, n=n, m=m, first=first, late=late, block=block, step=step),
+        functools.partial(late_kernel, n=n, m=m, groups=groups, block=block, step=step),
         [((1, n_rows), f32)] * n,
-        [VMEM] * (len(late) + 2),
+        [VMEM] * (len(ready) + len(late) + 1),
         [pltpu.VMEM((m, 1, n_rows), f32), pltpu.VMEM((len(late), n_rows, LANES), f32)],
-    )(early, *(grads[k] for k in late), train_store)
+    )(*ready, *(grads[k] for k in late), train_store)
     out = scores[0]
     for other in exchange(scores[1:], "seq", n, "scores"):
         out = out + other

time: 41.9 us -> 41.3 us (0.986)
  waiting for transfers between devices: 18.6 us -> 16.5 us
  starting transfers between devices: 16.3 us -> 17.8 us
    ppermute x12, waiting for transfers between devices: 18.6 us -> 16.5 us  [exchange(): got.append(lax.ppermute(arrays[i], axis, list(enumerate(route))))]
    ppermute x12, starting transfers between devices: 16.3 us -> 17.8 us  [exchange(): got.append(lax.ppermute(arrays[i], axis, list(enumerate(route))))]
    pallas_call x2 -> x3, Pallas kernels: 1.47 us -> 1.56 us  [the longest x2 1.15 us: body(): call(functools.partial(early_kernel, count=len(group), block=block, step=...]
  transfers between devices with their start and end apart: 12 -> 12, of which waited for: 9 -> 9; matrix products, arithmetic and copies ran while one was open for 0% -> 0% of each run, Pallas kernels for 8% -> 9%
where the time goes in v1:
time: 41.3 us; the launch traced here: 41.2 us
  starting transfers between devices  17.8 us (43%)
  waiting for transfers between devices  16.5 us (40%)
  Pallas kernels  5.57 us (13%)
  between operations  0.7 us (2%)
  other arithmetic  0.57 us (1%)
    ppermute x12, starting transfers between devices, exchange(): got.append(lax.ppermute(arrays[i], axis, list(enumerate(route))))  17.8 us
    ppermute x12, waiting for transfers between devices, exchange(): got.append(lax.ppermute(arrays[i], axis, list(enumerate(route))))  16.5 us
    pallas_call x1, Pallas kernels, body(): call(functools.partial(fetch_kernel, width=part), [(a.shape, a.dtype) for...  2.4 us
    pallas_call x2, Pallas kernels, body(): call(functools.partial(early_kernel, count=len(group), block=block, step=...  1.15 us
    pallas_call x1, Pallas kernels, body(): call(functools.partial(pack_kernel, n=n, width=part), [slices] * (n - 1),...  1.05 us
  transfers between devices with their start and end apart: 12, of which 9 were waited for; matrix products, arithmetic and copies ran while one was open for 0% of the time, Pallas kernels for 9%

profile of v1, /device:TPU:0, one launch (start us, length us, event | category | flops | bytes accessed | tf_op | source)
XLA Modules:
  0.0 41.2 jit_solution(17165945713138459980)
XLA Ops:
  0.0 1.1 %shard_map.64 = (bf16[2,32,1024]{2,1,0:T(8,128)(2,1)S(1)}, bf16[2,32,1024]{2,1,0:T(8,128)(2,1)S(1)}, bf16[2,32,1024]{2,1,0:T(8,128)(2,1)S(1)}) custom-call(bf16[1,32,4096]{2,1,0:T(8,128)(2,1)} %x.3, bf16[1,32,4096]{2,1,0:T(8,128)(2,1)} %g.3), custom_call_target="tpu_custom_call" | custom-call | tf_op jit(solution)/shard_map/pallas_call | solution.py:205
  1.1 5.1 %collective-permute-start = (bf16[2,32,1024]{2,1,0:T(8,128)(2,1)S(1)}, bf16[2,32,1024]{2,1,0:T(8,128)(2,1)S(1)}, u32[]{:S(2)}, u32[]{:S(2)}) collective-permute-start(bf16[2,32,1024]{2,1,0:T(8,128)(2,1)S(1)} %get-tuple-element.20.after), channel_id=1, source_target_pairs={{0,12},{4,8},{8,0},{12,4},{1,13},{5,9},{9,1},{13,5},{2,14},{6,10},... | collective-permute-start | bytes 393224 | tf_op jit(solution)/shard_map/ppermute | solution.py:51
  6.2 0.0 collective-permute-start.1
  6.2 0.9 %collective-permute-start.2 = (bf16[2,32,1024]{2,1,0:T(8,128)(2,1)S(1)}, bf16[2,32,1024]{2,1,0:T(8,128)(2,1)S(1)}, u32[]{:S(2)}, u32[]{:S(2)}) collective-permute-start(bf16[2,32,1024]{2,1,0:T(8,128)(2,1)S(1)} %get-tuple-element.23), channel_id=1, source_target_pairs={{0,4},{4,0},{8,12},{12,8},{1,5},{5,1},{9,13},{13,9},{2,6},{6,2},{1... | collective-permute-start | bytes 393224 | tf_op jit(solution)/shard_map/ppermute | solution.py:51
  7.1 2.4 %shard_map.65 = (bf16[1024,128]{1,0:T(8,128)(2,1)S(1)}, bf16[1024,128]{1,0:T(8,128)(2,1)S(1)}, f32[256,4096]{1,0:T(8,128)S(1)}, bf16[2,32,1024]{2,1,0:T(8,128)(2,1)S(1)}) custom-call(bf16[2,32,1024]{2,1,0:T(8,128)(2,1)S(1)} %get-tuple-element.20.after, bf16[1,32,4096]{2,1,0:T(8,128)(2,1)} %x.3, bf16[1,32,4096]{2,1,0:T(8,128)(2,1)} %g.3, ...), custom_call_target="tpu_custom_call" | custom-call | tf_op jit(solution)/shard_map/pallas_call | solution.py:212
  9.5 5.7 %collective-permute-done.refs_1_ = bf16[2,32,1024]{2,1,0:T(8,128)(2,1)S(1)} collective-permute-done((bf16[2,32,1024]{2,1,0:T(8,128)(2,1)S(1)}, bf16[2,32,1024]{2,1,0:T(8,128)(2,1)S(1)}, u32[]{:S(2)}, u32[]{:S(2)}) %collective-permute-start) | collective-permute-done | bytes 131104 | tf_op jit(solution)/shard_map/ppermute | solution.py:51
  15.2 0.0 collective-permute-done.1.refs_2_
  15.2 0.4 %collective-permute-done.2.refs_3_ = bf16[2,32,1024]{2,1,0:T(8,128)(2,1)S(1)} collective-permute-done((bf16[2,32,1024]{2,1,0:T(8,128)(2,1)S(1)}, bf16[2,32,1024]{2,1,0:T(8,128)(2,1)S(1)}, u32[]{:S(2)}, u32[]{:S(2)}) %collective-permute-start.2) | collective-permute-done | bytes 131104 | tf_op jit(solution)/shard_map/ppermute | solution.py:51
  15.6 0.4 shard_map.66
  16.0 1.6 %collective-permute-start.3 = (f32[160,128]{1,0:T(8,128)S(1)}, f32[160,128]{1,0:T(8,128)S(1)}, u32[]{:S(2)}, u32[]{:S(2)}) collective-permute-start(f32[160,128]{1,0:T(8,128)S(1)} %get-tuple-element.27), channel_id=1, source_target_pairs={{0,8},{4,12},{8,0},{12,4},{1,9},{5,13},{9,1},{13,5},{2,10},{6,14},... | collective-permute-start | bytes 245768 | tf_op jit(solution)/shard_map/ppermute | solution.py:51
  17.6 3.1 %collective-permute-start.4 = (f32[160,128]{1,0:T(8,128)S(1)}, f32[160,128]{1,0:T(8,128)S(1)}, u32[]{:S(2)}, u32[]{:S(2)}) collective-permute-start(f32[160,128]{1,0:T(8,128)S(1)} %get-tuple-element.28), channel_id=1, source_target_pairs={{0,4},{4,8},{8,12},{12,0},{1,5},{5,9},{9,13},{13,1},{2,6},{6,10},{... | collective-permute-start | bytes 245768 | tf_op jit(solution)/shard_map/ppermute | solution.py:51
  20.8 0.7 %collective-permute-start.5 = (f32[160,128]{1,0:T(8,128)S(1)}, f32[160,128]{1,0:T(8,128)S(1)}, u32[]{:S(2)}, u32[]{:S(2)}) collective-permute-start(f32[160,128]{1,0:T(8,128)S(1)} %get-tuple-element.29), channel_id=1, source_target_pairs={{0,12},{4,0},{8,4},{12,8},{1,13},{5,1},{9,5},{13,9},{2,14},{6,2},{... | collective-permute-start | bytes 245768 | tf_op jit(solution)/shard_map/ppermute | solution.py:51
  22.1 3.4 %collective-permute-done.3.refs_1_ = f32[160,128]{1,0:T(8,128)S(1)} collective-permute-done((f32[160,128]{1,0:T(8,128)S(1)}, f32[160,128]{1,0:T(8,128)S(1)}, u32[]{:S(2)}, u32[]{:S(2)}) %collective-permute-start.3) | collective-permute-done | bytes 81952 | tf_op jit(solution)/shard_map/ppermute | solution.py:51
  25.5 0.0 collective-permute-done.4.refs_2_
  25.5 0.5 %collective-permute-done.5.refs_3_ = f32[160,128]{1,0:T(8,128)S(1)} collective-permute-done((f32[160,128]{1,0:T(8,128)S(1)}, f32[160,128]{1,0:T(8,128)S(1)}, u32[]{:S(2)}, u32[]{:S(2)}) %collective-permute-start.5) | collective-permute-done | bytes 81952 | tf_op jit(solution)/shard_map/ppermute | solution.py:51
  26.0 0.2 shard_map.67.refs_0_
  26.2 0.0 collective-permute-start.6
  26.2 1.4 %collective-permute-start.7 = (f32[32,128]{1,0:T(8,128)S(1)}, f32[32,128]{1,0:T(8,128)S(1)}, u32[]{:S(2)}, u32[]{:S(2)}) collective-permute-start(f32[32,128]{1,0:T(8,128)S(1)} %shard_map.67.refs_0_), channel_id=1, source_target_pairs={{0,3},{1,2},{2,1},{3,0},{4,7},{5,6},{6,5},{7,4},{8,11},{9,10},{10,... | collective-permute-start | bytes 49160 | tf_op jit(solution)/shard_map/ppermute | solution.py:51
  27.6 0.8 %collective-permute-start.8 = (f32[32,128]{1,0:T(8,128)S(1)}, f32[32,128]{1,0:T(8,128)S(1)}, u32[]{:S(2)}, u32[]{:S(2)}) collective-permute-start(f32[32,128]{1,0:T(8,128)S(1)} %shard_map.67.refs_0_), channel_id=1, source_target_pairs={{0,2},{1,3},{2,0},{3,1},{4,6},{5,7},{6,4},{7,5},{8,10},{9,11},{10,... | collective-permute-start | bytes 49160 | tf_op jit(solution)/shard_map/ppermute | solution.py:51
  28.4 0.0 collective-permute-done.6.refs_1_
  28.4 0.8 %shard_map.68.refs_1_.refs_0_ = f32[2,1,256]{2,1,0:T(1,128)S(1)} custom-call(f32[32,128]{1,0:T(8,128)S(1)} %shard_map.67.refs_0_, f32[32,128]{1,0:T(8,128)S(1)} %collective-permute-done.6.refs_1_, f32[256,4096]{1,0:T(8,128)S(1)} %get-tuple-element.30.refs_2_.refs_3_), custom_call_target="tpu_custom_call" | custom-call | tf_op jit(solution)/shard_map/pallas_call | solution.py:239
  29.1 0.3 collective-permute-done.7.refs_0_
  29.4 0.4 shard_map.69.refs_1_
  29.8 1.5 %collective-permute-done.8.refs_2_ = f32[32,128]{1,0:T(8,128)S(1)} collective-permute-done((f32[32,128]{1,0:T(8,128)S(1)}, f32[32,128]{1,0:T(8,128)S(1)}, u32[]{:S(2)}, u32[]{:S(2)}) %collective-permute-start.8) | collective-permute-done | bytes 16416 | tf_op jit(solution)/shard_map/ppermute | solution.py:51
  31.3 0.4 shard_map.70
  31.7 2.2 %collective-permute-start.10 = (f32[1,256]{1,0:T(1,128)S(1)}, f32[1,256]{1,0:T(1,128)S(1)}, u32[]{:S(2)}, u32[]{:S(2)}) collective-permute-start(f32[1,256]{1,0:T(1,128)S(1)} %get-tuple-element.33), channel_id=1, source_target_pairs={{0,8},{4,12},{8,0},{12,4},{1,9},{5,13},{9,1},{13,5},{2,10},{6,14},... | collective-permute-start | bytes 3080 | tf_op jit(solution)/shard_map/ppermute | solution.py:51
  33.9 1.3 %collective-permute-start.11 = (f32[1,256]{1,0:T(1,128)S(1)}, f32[1,256]{1,0:T(1,128)S(1)}, u32[]{:S(2)}, u32[]{:S(2)}) collective-permute-start(f32[1,256]{1,0:T(1,128)S(1)} %get-tuple-element.34), channel_id=1, source_target_pairs={{0,12},{4,0},{8,4},{12,8},{1,13},{5,1},{9,5},{13,9},{2,14},{6,2},{... | collective-permute-start | bytes 3080 | tf_op jit(solution)/shard_map/ppermute | solution.py:51
  35.2 0.7 %collective-permute-start.9 = (f32[1,256]{1,0:T(1,128)S(1)}, f32[1,256]{1,0:T(1,128)S(1)}, u32[]{:S(2)}, u32[]{:S(2)}) collective-permute-start(f32[1,256]{1,0:T(1,128)S(1)} %get-tuple-element.32), channel_id=1, source_target_pairs={{0,4},{4,8},{8,12},{12,0},{1,5},{5,9},{9,13},{13,1},{2,6},{6,10},{... | collective-permute-start | bytes 3080 | tf_op jit(solution)/shard_map/ppermute | solution.py:51
  35.9 0.3 collective-permute-done.10
  36.3 1.2 %collective-permute-done.11 = f32[1,256]{1,0:T(1,128)S(1)} collective-permute-done((f32[1,256]{1,0:T(1,128)S(1)}, f32[1,256]{1,0:T(1,128)S(1)}, u32[]{:S(2)}, u32[]{:S(2)}) %collective-permute-start.11) | collective-permute-done | bytes 1056 | tf_op jit(solution)/shard_map/ppermute | solution.py:51
  37.5 3.1 %collective-permute-done.9 = f32[1,256]{1,0:T(1,128)S(1)} collective-permute-done((f32[1,256]{1,0:T(1,128)S(1)}, f32[1,256]{1,0:T(1,128)S(1)}, u32[]{:S(2)}, u32[]{:S(2)}) %collective-permute-start.9) | collective-permute-done | bytes 1056 | tf_op jit(solution)/shard_map/ppermute | solution.py:51
  40.6 0.6 %add_add_fusion = f32[1,256]{1,0:T(1,128)} fusion(f32[1,256]{1,0:T(1,128)S(1)} %collective-permute-done.11, f32[1,256]{1,0:T(1,128)S(1)} %collective-permute-done.10, f32[1,256]{1,0:T(1,128)S(1)} %get-tuple-element.31, f32[1,256]{1,0:T(1,128)S(1)} %collective-permute-done.9), kind=kLoop, calls=%fused_computation | loop fusion | flops 768 | bytes 5120 | tf_op jit(solution)/shard_map/add | solution.py:255
Async XLA Ops:
  1.1 14.1 %collective-permute-start = (bf16[2,32,1024]{2,1,0:T(8,128)(2,1)S(1)}, bf16[2,32,1024]{2,1,0:T(8,128)(2,1)S(1)}, u32[]{:S(2)}, u32[]{:S(2)}) collective-permute-start(bf16[2,32,1024]{2,1,0:T(8,128)(2,1)S(1)} %get-tuple-element.20.after), channel_id=1, source_target_pairs={{0,12},{4,8},{8,0},{12,4},{1,13},{5,9},{9,1},{13,5},{2,14},{6,10},... | collective-permute-start | bytes 393224 | tf_op jit(solution)/shard_map/ppermute | solution.py:51
  6.2 9.0 %collective-permute-start.1 = (bf16[2,32,1024]{2,1,0:T(8,128)(2,1)S(1)}, bf16[2,32,1024]{2,1,0:T(8,128)(2,1)S(1)}, u32[]{:S(2)}, u32[]{:S(2)}) collective-permute-start(bf16[2,32,1024]{2,1,0:T(8,128)(2,1)S(1)} %get-tuple-element.22), channel_id=1, source_target_pairs={{0,8},{4,12},{8,4},{12,0},{1,9},{5,13},{9,5},{13,1},{2,10},{6,14},... | collective-permute-start | bytes 393224 | tf_op jit(solution)/shard_map/ppermute | solution.py:51
  6.2 9.4 %collective-permute-start.2 = (bf16[2,32,1024]{2,1,0:T(8,128)(2,1)S(1)}, bf16[2,32,1024]{2,1,0:T(8,128)(2,1)S(1)}, u32[]{:S(2)}, u32[]{:S(2)}) collective-permute-start(bf16[2,32,1024]{2,1,0:T(8,128)(2,1)S(1)} %get-tuple-element.23), channel_id=1, source_target_pairs={{0,4},{4,0},{8,12},{12,8},{1,5},{5,1},{9,13},{13,9},{2,6},{6,2},{1... | collective-permute-start | bytes 393224 | tf_op jit(solution)/shard_map/ppermute | solution.py:51
  16.0 9.5 %collective-permute-start.3 = (f32[160,128]{1,0:T(8,128)S(1)}, f32[160,128]{1,0:T(8,128)S(1)}, u32[]{:S(2)}, u32[]{:S(2)}) collective-permute-start(f32[160,128]{1,0:T(8,128)S(1)} %get-tuple-element.27), channel_id=1, source_target_pairs={{0,8},{4,12},{8,0},{12,4},{1,9},{5,13},{9,1},{13,5},{2,10},{6,14},... | collective-permute-start | bytes 245768 | tf_op jit(solution)/shard_map/ppermute | solution.py:51
  17.6 7.9 %collective-permute-start.4 = (f32[160,128]{1,0:T(8,128)S(1)}, f32[160,128]{1,0:T(8,128)S(1)}, u32[]{:S(2)}, u32[]{:S(2)}) collective-permute-start(f32[160,128]{1,0:T(8,128)S(1)} %get-tuple-element.28), channel_id=1, source_target_pairs={{0,4},{4,8},{8,12},{12,0},{1,5},{5,9},{9,13},{13,1},{2,6},{6,10},{... | collective-permute-start | bytes 245768 | tf_op jit(solution)/shard_map/ppermute | solution.py:51
  20.8 5.3 %collective-permute-start.5 = (f32[160,128]{1,0:T(8,128)S(1)}, f32[160,128]{1,0:T(8,128)S(1)}, u32[]{:S(2)}, u32[]{:S(2)}) collective-permute-start(f32[160,128]{1,0:T(8,128)S(1)} %get-tuple-element.29), channel_id=1, source_target_pairs={{0,12},{4,0},{8,4},{12,8},{1,13},{5,1},{9,5},{13,9},{2,14},{6,2},{... | collective-permute-start | bytes 245768 | tf_op jit(solution)/shard_map/ppermute | solution.py:51
  26.2 2.2 %collective-permute-start.6 = (f32[32,128]{1,0:T(8,128)S(1)}, f32[32,128]{1,0:T(8,128)S(1)}, u32[]{:S(2)}, u32[]{:S(2)}) collective-permute-start(f32[32,128]{1,0:T(8,128)S(1)} %shard_map.67.refs_0_), channel_id=1, source_target_pairs={{0,1},{1,0},{2,3},{3,2},{4,5},{5,4},{6,7},{7,6},{8,9},{9,8},{10,11... | collective-permute-start | bytes 49160 | tf_op jit(solution)/shard_map/ppermute | solution.py:51
  26.2 3.2 %collective-permute-start.7 = (f32[32,128]{1,0:T(8,128)S(1)}, f32[32,128]{1,0:T(8,128)S(1)}, u32[]{:S(2)}, u32[]{:S(2)}) collective-permute-start(f32[32,128]{1,0:T(8,128)S(1)} %shard_map.67.refs_0_), channel_id=1, source_target_pairs={{0,3},{1,2},{2,1},{3,0},{4,7},{5,6},{6,5},{7,4},{8,11},{9,10},{10,... | collective-permute-start | bytes 49160 | tf_op jit(solution)/shard_map/ppermute | solution.py:51
  27.6 3.7 %collective-permute-start.8 = (f32[32,128]{1,0:T(8,128)S(1)}, f32[32,128]{1,0:T(8,128)S(1)}, u32[]{:S(2)}, u32[]{:S(2)}) collective-permute-start(f32[32,128]{1,0:T(8,128)S(1)} %shard_map.67.refs_0_), channel_id=1, source_target_pairs={{0,2},{1,3},{2,0},{3,1},{4,6},{5,7},{6,4},{7,5},{8,10},{9,11},{10,... | collective-permute-start | bytes 49160 | tf_op jit(solution)/shard_map/ppermute | solution.py:51
  31.7 4.5 %collective-permute-start.10 = (f32[1,256]{1,0:T(1,128)S(1)}, f32[1,256]{1,0:T(1,128)S(1)}, u32[]{:S(2)}, u32[]{:S(2)}) collective-permute-start(f32[1,256]{1,0:T(1,128)S(1)} %get-tuple-element.33), channel_id=1, source_target_pairs={{0,8},{4,12},{8,0},{12,4},{1,9},{5,13},{9,1},{13,5},{2,10},{6,14},... | collective-permute-start | bytes 3080 | tf_op jit(solution)/shard_map/ppermute | solution.py:51
  33.9 3.6 %collective-permute-start.11 = (f32[1,256]{1,0:T(1,128)S(1)}, f32[1,256]{1,0:T(1,128)S(1)}, u32[]{:S(2)}, u32[]{:S(2)}) collective-permute-start(f32[1,256]{1,0:T(1,128)S(1)} %get-tuple-element.34), channel_id=1, source_target_pairs={{0,12},{4,0},{8,4},{12,8},{1,13},{5,1},{9,5},{13,9},{2,14},{6,2},{... | collective-permute-start | bytes 3080 | tf_op jit(solution)/shard_map/ppermute | solution.py:51
  35.2 5.4 %collective-permute-start.9 = (f32[1,256]{1,0:T(1,128)S(1)}, f32[1,256]{1,0:T(1,128)S(1)}, u32[]{:S(2)}, u32[]{:S(2)}) collective-permute-start(f32[1,256]{1,0:T(1,128)S(1)} %get-tuple-element.32), channel_id=1, source_target_pairs={{0,4},{4,8},{8,12},{12,0},{1,5},{5,9},{9,13},{13,1},{2,6},{6,10},{... | collective-permute-start | bytes 3080 | tf_op jit(solution)/shard_map/ppermute | solution.py:51

commit v2 on v1

--- a/solution.py
+++ b/solution.py
@@ -113,10 +113,12 @@
         for j in range(2):
             rows[j, pl.ds(at, n_tok), :] = toks[k][j]
     first = jnp.dot(rows[0], w_in[...], preferred_element_type=jnp.float32)
-    second = jnp.dot(rows[1], w_out[...], preferred_element_type=jnp.float32)
+    outT = lax.dot_general(
+        w_out[...], rows[1], (((0,), (1,)), ((), ())), preferred_element_type=jnp.float32
+    )
     turned = refs[2 * n + 3]
     for c in range(total // LANES):
-        turned[c] = second[c * LANES : (c + 1) * LANES].T
+        turned[c] = outT[:, c * LANES : (c + 1) * LANES]
     for k in range(n):
         at = pl.multiple_of(to[k] * block, block)
         outs[k][:total] = first
@@ -233,7 +235,7 @@
     )(query_lengths, *parts)
     grads = [grad] + exchange([grad] * (m - 1), "rows", m, "gradient")
 
-    groups = ((0, m - 1), tuple(range(1, m // 2)), tuple(range(m // 2, m - 1)))
+    groups = ((0,), (m - 1,), tuple(range(1, m // 2)), tuple(range(m // 2, m - 1)))
     ready = []
     for group in groups[:-1]:
         ready += call(

time: 41.3 us -> 41.2 us (level)
    pallas_call x2 -> x3, Pallas kernels: 1.15 us -> 1.12 us  [body(): call(functools.partial(early_kernel, count=len(group), block=block, step=...]
where the time goes in v2:
time: 41.2 us; the launch traced here: 41.1 us
  starting transfers between devices  17.8 us (43%)
  waiting for transfers between devices  16.5 us (40%)
  Pallas kernels  5.44 us (13%)
  between operations  0.69 us (2%)
  other arithmetic  0.57 us (1%)
    ppermute x12, starting transfers between devices, exchange(): got.append(lax.ppermute(arrays[i], axis, list(enumerate(route))))  17.8 us
    ppermute x12, waiting for transfers between devices, exchange(): got.append(lax.ppermute(arrays[i], axis, list(enumerate(route))))  16.5 us
    pallas_call x1, Pallas kernels, body(): call(functools.partial(fetch_kernel, width=part), [(a.shape, a.dtype) for...  2.4 us
    pallas_call x3, Pallas kernels, body(): call(functools.partial(early_kernel, count=len(group), block=block, step=...  1.12 us
    pallas_call x1, Pallas kernels, body(): call(functools.partial(pack_kernel, n=n, width=part), [slices] * (n - 1),...  1.05 us
  transfers between devices with their start and end apart: 12, of which 9 were waited for; matrix products, arithmetic and copies ran while one was open for 0% of the time, Pallas kernels for 9%

profile of v2, /device:TPU:0, one launch (start us, length us, event | category | flops | bytes accessed | tf_op | source)
XLA Modules:
  0.0 41.1 jit_solution(7364542390110134617)
XLA Ops:
  0.0 1.1 %shard_map.64 = (bf16[2,32,1024]{2,1,0:T(8,128)(2,1)S(1)}, bf16[2,32,1024]{2,1,0:T(8,128)(2,1)S(1)}, bf16[2,32,1024]{2,1,0:T(8,128)(2,1)S(1)}) custom-call(bf16[1,32,4096]{2,1,0:T(8,128)(2,1)} %x.3, bf16[1,32,4096]{2,1,0:T(8,128)(2,1)} %g.3), custom_call_target="tpu_custom_call" | custom-call | tf_op jit(solution)/shard_map/pallas_call | solution.py:207
  1.1 5.1 %collective-permute-start = (bf16[2,32,1024]{2,1,0:T(8,128)(2,1)S(1)}, bf16[2,32,1024]{2,1,0:T(8,128)(2,1)S(1)}, u32[]{:S(2)}, u32[]{:S(2)}) collective-permute-start(bf16[2,32,1024]{2,1,0:T(8,128)(2,1)S(1)} %get-tuple-element.20.after), channel_id=1, source_target_pairs={{0,12},{4,8},{8,0},{12,4},{1,13},{5,9},{9,1},{13,5},{2,14},{6,10},... | collective-permute-start | bytes 393224 | tf_op jit(solution)/shard_map/ppermute | solution.py:51
  6.2 0.0 collective-permute-start.1
  6.2 0.9 %collective-permute-start.2 = (bf16[2,32,1024]{2,1,0:T(8,128)(2,1)S(1)}, bf16[2,32,1024]{2,1,0:T(8,128)(2,1)S(1)}, u32[]{:S(2)}, u32[]{:S(2)}) collective-permute-start(bf16[2,32,1024]{2,1,0:T(8,128)(2,1)S(1)} %get-tuple-element.23), channel_id=1, source_target_pairs={{0,4},{4,0},{8,12},{12,8},{1,5},{5,1},{9,13},{13,9},{2,6},{6,2},{1... | collective-permute-start | bytes 393224 | tf_op jit(solution)/shard_map/ppermute | solution.py:51
  7.1 2.4 %shard_map.65 = (bf16[1024,128]{1,0:T(8,128)(2,1)S(1)}, bf16[1024,128]{1,0:T(8,128)(2,1)S(1)}, f32[256,4096]{1,0:T(8,128)S(1)}, bf16[2,32,1024]{2,1,0:T(8,128)(2,1)S(1)}) custom-call(bf16[2,32,1024]{2,1,0:T(8,128)(2,1)S(1)} %get-tuple-element.20.after, bf16[1,32,4096]{2,1,0:T(8,128)(2,1)} %x.3, bf16[1,32,4096]{2,1,0:T(8,128)(2,1)} %g.3, ...), custom_call_target="tpu_custom_call" | custom-call | tf_op jit(solution)/shard_map/pallas_call | solution.py:214
  9.5 5.7 %collective-permute-done.refs_1_ = bf16[2,32,1024]{2,1,0:T(8,128)(2,1)S(1)} collective-permute-done((bf16[2,32,1024]{2,1,0:T(8,128)(2,1)S(1)}, bf16[2,32,1024]{2,1,0:T(8,128)(2,1)S(1)}, u32[]{:S(2)}, u32[]{:S(2)}) %collective-permute-start) | collective-permute-done | bytes 131104 | tf_op jit(solution)/shard_map/ppermute | solution.py:51
  15.2 0.0 collective-permute-done.1.refs_2_
  15.2 0.4 %collective-permute-done.2.refs_3_ = bf16[2,32,1024]{2,1,0:T(8,128)(2,1)S(1)} collective-permute-done((bf16[2,32,1024]{2,1,0:T(8,128)(2,1)S(1)}, bf16[2,32,1024]{2,1,0:T(8,128)(2,1)S(1)}, u32[]{:S(2)}, u32[]{:S(2)}) %collective-permute-start.2) | collective-permute-done | bytes 131104 | tf_op jit(solution)/shard_map/ppermute | solution.py:51
  15.6 0.3 shard_map.66
  15.9 1.6 %collective-permute-start.3 = (f32[160,128]{1,0:T(8,128)S(1)}, f32[160,128]{1,0:T(8,128)S(1)}, u32[]{:S(2)}, u32[]{:S(2)}) collective-permute-start(f32[160,128]{1,0:T(8,128)S(1)} %get-tuple-element.27), channel_id=1, source_target_pairs={{0,8},{4,12},{8,0},{12,4},{1,9},{5,13},{9,1},{13,5},{2,10},{6,14},... | collective-permute-start | bytes 245768 | tf_op jit(solution)/shard_map/ppermute | solution.py:51
  17.6 3.1 %collective-permute-start.4 = (f32[160,128]{1,0:T(8,128)S(1)}, f32[160,128]{1,0:T(8,128)S(1)}, u32[]{:S(2)}, u32[]{:S(2)}) collective-permute-start(f32[160,128]{1,0:T(8,128)S(1)} %get-tuple-element.28), channel_id=1, source_target_pairs={{0,4},{4,8},{8,12},{12,0},{1,5},{5,9},{9,13},{13,1},{2,6},{6,10},{... | collective-permute-start | bytes 245768 | tf_op jit(solution)/shard_map/ppermute | solution.py:51
  20.7 0.7 %collective-permute-start.5 = (f32[160,128]{1,0:T(8,128)S(1)}, f32[160,128]{1,0:T(8,128)S(1)}, u32[]{:S(2)}, u32[]{:S(2)}) collective-permute-start(f32[160,128]{1,0:T(8,128)S(1)} %get-tuple-element.29), channel_id=1, source_target_pairs={{0,12},{4,0},{8,4},{12,8},{1,13},{5,1},{9,5},{13,9},{2,14},{6,2},{... | collective-permute-start | bytes 245768 | tf_op jit(solution)/shard_map/ppermute | solution.py:51
  22.0 3.4 %collective-permute-done.3.refs_1_ = f32[160,128]{1,0:T(8,128)S(1)} collective-permute-done((f32[160,128]{1,0:T(8,128)S(1)}, f32[160,128]{1,0:T(8,128)S(1)}, u32[]{:S(2)}, u32[]{:S(2)}) %collective-permute-start.3) | collective-permute-done | bytes 81952 | tf_op jit(solution)/shard_map/ppermute | solution.py:51
  25.5 0.0 collective-permute-done.4.refs_2_
  25.5 0.5 %collective-permute-done.5.refs_3_ = f32[160,128]{1,0:T(8,128)S(1)} collective-permute-done((f32[160,128]{1,0:T(8,128)S(1)}, f32[160,128]{1,0:T(8,128)S(1)}, u32[]{:S(2)}, u32[]{:S(2)}) %collective-permute-start.5) | collective-permute-done | bytes 81952 | tf_op jit(solution)/shard_map/ppermute | solution.py:51
  26.0 0.2 shard_map.67.refs_0_
  26.1 0.0 collective-permute-start.6
  26.1 1.4 %collective-permute-start.7 = (f32[32,128]{1,0:T(8,128)S(1)}, f32[32,128]{1,0:T(8,128)S(1)}, u32[]{:S(2)}, u32[]{:S(2)}) collective-permute-start(f32[32,128]{1,0:T(8,128)S(1)} %shard_map.67.refs_0_), channel_id=1, source_target_pairs={{0,3},{1,2},{2,1},{3,0},{4,7},{5,6},{6,5},{7,4},{8,11},{9,10},{10,... | collective-permute-start | bytes 49160 | tf_op jit(solution)/shard_map/ppermute | solution.py:51
  27.5 0.7 %collective-permute-start.8 = (f32[32,128]{1,0:T(8,128)S(1)}, f32[32,128]{1,0:T(8,128)S(1)}, u32[]{:S(2)}, u32[]{:S(2)}) collective-permute-start(f32[32,128]{1,0:T(8,128)S(1)} %shard_map.67.refs_0_), channel_id=1, source_target_pairs={{0,2},{1,3},{2,0},{3,1},{4,6},{5,7},{6,4},{7,5},{8,10},{9,11},{10,... | collective-permute-start | bytes 49160 | tf_op jit(solution)/shard_map/ppermute | solution.py:51
  28.3 0.4 shard_map.68.refs_1_.refs_0_
  28.7 0.4 shard_map.69.refs_2_.refs_1_
  29.0 0.3 collective-permute-done.7.refs_0_
  29.3 0.4 shard_map.70.refs_2_
  29.7 1.6 %collective-permute-done.8.refs_3_ = f32[32,128]{1,0:T(8,128)S(1)} collective-permute-done((f32[32,128]{1,0:T(8,128)S(1)}, f32[32,128]{1,0:T(8,128)S(1)}, u32[]{:S(2)}, u32[]{:S(2)}) %collective-permute-start.8) | collective-permute-done | bytes 16416 | tf_op jit(solution)/shard_map/ppermute | solution.py:51
  31.3 0.4 shard_map.71
  31.7 2.2 %collective-permute-start.10 = (f32[1,256]{1,0:T(1,128)S(1)}, f32[1,256]{1,0:T(1,128)S(1)}, u32[]{:S(2)}, u32[]{:S(2)}) collective-permute-start(f32[1,256]{1,0:T(1,128)S(1)} %get-tuple-element.33), channel_id=1, source_target_pairs={{0,8},{4,12},{8,0},{12,4},{1,9},{5,13},{9,1},{13,5},{2,10},{6,14},... | collective-permute-start | bytes 3080 | tf_op jit(solution)/shard_map/ppermute | solution.py:51
  33.8 1.3 %collective-permute-start.11 = (f32[1,256]{1,0:T(1,128)S(1)}, f32[1,256]{1,0:T(1,128)S(1)}, u32[]{:S(2)}, u32[]{:S(2)}) collective-permute-start(f32[1,256]{1,0:T(1,128)S(1)} %get-tuple-element.34), channel_id=1, source_target_pairs={{0,12},{4,0},{8,4},{12,8},{1,13},{5,1},{9,5},{13,9},{2,14},{6,2},{... | collective-permute-start | bytes 3080 | tf_op jit(solution)/shard_map/ppermute | solution.py:51
  35.1 0.7 %collective-permute-start.9 = (f32[1,256]{1,0:T(1,128)S(1)}, f32[1,256]{1,0:T(1,128)S(1)}, u32[]{:S(2)}, u32[]{:S(2)}) collective-permute-start(f32[1,256]{1,0:T(1,128)S(1)} %get-tuple-element.32), channel_id=1, source_target_pairs={{0,4},{4,8},{8,12},{12,0},{1,5},{5,9},{9,13},{13,1},{2,6},{6,10},{... | collective-permute-start | bytes 3080 | tf_op jit(solution)/shard_map/ppermute | solution.py:51
  35.8 0.3 collective-permute-done.10
  36.2 1.2 %collective-permute-done.11 = f32[1,256]{1,0:T(1,128)S(1)} collective-permute-done((f32[1,256]{1,0:T(1,128)S(1)}, f32[1,256]{1,0:T(1,128)S(1)}, u32[]{:S(2)}, u32[]{:S(2)}) %collective-permute-start.11) | collective-permute-done | bytes 1056 | tf_op jit(solution)/shard_map/ppermute | solution.py:51
  37.4 3.1 %collective-permute-done.9 = f32[1,256]{1,0:T(1,128)S(1)} collective-permute-done((f32[1,256]{1,0:T(1,128)S(1)}, f32[1,256]{1,0:T(1,128)S(1)}, u32[]{:S(2)}, u32[]{:S(2)}) %collective-permute-start.9) | collective-permute-done | bytes 1056 | tf_op jit(solution)/shard_map/ppermute | solution.py:51
  40.5 0.6 %add_add_fusion = f32[1,256]{1,0:T(1,128)} fusion(f32[1,256]{1,0:T(1,128)S(1)} %collective-permute-done.11, f32[1,256]{1,0:T(1,128)S(1)} %collective-permute-done.10, f32[1,256]{1,0:T(1,128)S(1)} %get-tuple-element.31, f32[1,256]{1,0:T(1,128)S(1)} %collective-permute-done.9), kind=kLoop, calls=%fused_computation | loop fusion | flops 768 | bytes 5120 | tf_op jit(solution)/shard_map/add | solution.py:257
  (1 shorter events, 0.0 us)
Async XLA Ops:
  1.1 14.1 %collective-permute-start = (bf16[2,32,1024]{2,1,0:T(8,128)(2,1)S(1)}, bf16[2,32,1024]{2,1,0:T(8,128)(2,1)S(1)}, u32[]{:S(2)}, u32[]{:S(2)}) collective-permute-start(bf16[2,32,1024]{2,1,0:T(8,128)(2,1)S(1)} %get-tuple-element.20.after), channel_id=1, source_target_pairs={{0,12},{4,8},{8,0},{12,4},{1,13},{5,9},{9,1},{13,5},{2,14},{6,10},... | collective-permute-start | bytes 393224 | tf_op jit(solution)/shard_map/ppermute | solution.py:51
  6.2 9.0 %collective-permute-start.1 = (bf16[2,32,1024]{2,1,0:T(8,128)(2,1)S(1)}, bf16[2,32,1024]{2,1,0:T(8,128)(2,1)S(1)}, u32[]{:S(2)}, u32[]{:S(2)}) collective-permute-start(bf16[2,32,1024]{2,1,0:T(8,128)(2,1)S(1)} %get-tuple-element.22), channel_id=1, source_target_pairs={{0,8},{4,12},{8,4},{12,0},{1,9},{5,13},{9,5},{13,1},{2,10},{6,14},... | collective-permute-start | bytes 393224 | tf_op jit(solution)/shard_map/ppermute | solution.py:51
  6.2 9.4 %collective-permute-start.2 = (bf16[2,32,1024]{2,1,0:T(8,128)(2,1)S(1)}, bf16[2,32,1024]{2,1,0:T(8,128)(2,1)S(1)}, u32[]{:S(2)}, u32[]{:S(2)}) collective-permute-start(bf16[2,32,1024]{2,1,0:T(8,128)(2,1)S(1)} %get-tuple-element.23), channel_id=1, source_target_pairs={{0,4},{4,0},{8,12},{12,8},{1,5},{5,1},{9,13},{13,9},{2,6},{6,2},{1... | collective-permute-start | bytes 393224 | tf_op jit(solution)/shard_map/ppermute | solution.py:51
  15.9 9.5 %collective-permute-start.3 = (f32[160,128]{1,0:T(8,128)S(1)}, f32[160,128]{1,0:T(8,128)S(1)}, u32[]{:S(2)}, u32[]{:S(2)}) collective-permute-start(f32[160,128]{1,0:T(8,128)S(1)} %get-tuple-element.27), channel_id=1, source_target_pairs={{0,8},{4,12},{8,0},{12,4},{1,9},{5,13},{9,1},{13,5},{2,10},{6,14},... | collective-permute-start | bytes 245768 | tf_op jit(solution)/shard_map/ppermute | solution.py:51
  17.6 7.9 %collective-permute-start.4 = (f32[160,128]{1,0:T(8,128)S(1)}, f32[160,128]{1,0:T(8,128)S(1)}, u32[]{:S(2)}, u32[]{:S(2)}) collective-permute-start(f32[160,128]{1,0:T(8,128)S(1)} %get-tuple-element.28), channel_id=1, source_target_pairs={{0,4},{4,8},{8,12},{12,0},{1,5},{5,9},{9,13},{13,1},{2,6},{6,10},{... | collective-permute-start | bytes 245768 | tf_op jit(solution)/shard_map/ppermute | solution.py:51
  20.7 5.3 %collective-permute-start.5 = (f32[160,128]{1,0:T(8,128)S(1)}, f32[160,128]{1,0:T(8,128)S(1)}, u32[]{:S(2)}, u32[]{:S(2)}) collective-permute-start(f32[160,128]{1,0:T(8,128)S(1)} %get-tuple-element.29), channel_id=1, source_target_pairs={{0,12},{4,0},{8,4},{12,8},{1,13},{5,1},{9,5},{13,9},{2,14},{6,2},{... | collective-permute-start | bytes 245768 | tf_op jit(solution)/shard_map/ppermute | solution.py:51
  26.1 2.5 %collective-permute-start.6 = (f32[32,128]{1,0:T(8,128)S(1)}, f32[32,128]{1,0:T(8,128)S(1)}, u32[]{:S(2)}, u32[]{:S(2)}) collective-permute-start(f32[32,128]{1,0:T(8,128)S(1)} %shard_map.67.refs_0_), channel_id=1, source_target_pairs={{0,1},{1,0},{2,3},{3,2},{4,5},{5,4},{6,7},{7,6},{8,9},{9,8},{10,11... | collective-permute-start | bytes 49160 | tf_op jit(solution)/shard_map/ppermute | solution.py:51
  26.1 3.2 %collective-permute-start.7 = (f32[32,128]{1,0:T(8,128)S(1)}, f32[32,128]{1,0:T(8,128)S(1)}, u32[]{:S(2)}, u32[]{:S(2)}) collective-permute-start(f32[32,128]{1,0:T(8,128)S(1)} %shard_map.67.refs_0_), channel_id=1, source_target_pairs={{0,3},{1,2},{2,1},{3,0},{4,7},{5,6},{6,5},{7,4},{8,11},{9,10},{10,... | collective-permute-start | bytes 49160 | tf_op jit(solution)/shard_map/ppermute | solution.py:51
  27.5 3.7 %collective-permute-start.8 = (f32[32,128]{1,0:T(8,128)S(1)}, f32[32,128]{1,0:T(8,128)S(1)}, u32[]{:S(2)}, u32[]{:S(2)}) collective-permute-start(f32[32,128]{1,0:T(8,128)S(1)} %shard_map.67.refs_0_), channel_id=1, source_target_pairs={{0,2},{1,3},{2,0},{3,1},{4,6},{5,7},{6,4},{7,5},{8,10},{9,11},{10,... | collective-permute-start | bytes 49160 | tf_op jit(solution)/shard_map/ppermute | solution.py:51
  31.7 4.5 %collective-permute-start.10 = (f32[1,256]{1,0:T(1,128)S(1)}, f32[1,256]{1,0:T(1,128)S(1)}, u32[]{:S(2)}, u32[]{:S(2)}) collective-permute-start(f32[1,256]{1,0:T(1,128)S(1)} %get-tuple-element.33), channel_id=1, source_target_pairs={{0,8},{4,12},{8,0},{12,4},{1,9},{5,13},{9,1},{13,5},{2,10},{6,14},... | collective-permute-start | bytes 3080 | tf_op jit(solution)/shard_map/ppermute | solution.py:51
  33.8 3.6 %collective-permute-start.11 = (f32[1,256]{1,0:T(1,128)S(1)}, f32[1,256]{1,0:T(1,128)S(1)}, u32[]{:S(2)}, u32[]{:S(2)}) collective-permute-start(f32[1,256]{1,0:T(1,128)S(1)} %get-tuple-element.34), channel_id=1, source_target_pairs={{0,12},{4,0},{8,4},{12,8},{1,13},{5,1},{9,5},{13,9},{2,14},{6,2},{... | collective-permute-start | bytes 3080 | tf_op jit(solution)/shard_map/ppermute | solution.py:51
  35.1 5.4 %collective-permute-start.9 = (f32[1,256]{1,0:T(1,128)S(1)}, f32[1,256]{1,0:T(1,128)S(1)}, u32[]{:S(2)}, u32[]{:S(2)}) collective-permute-start(f32[1,256]{1,0:T(1,128)S(1)} %get-tuple-element.32), channel_id=1, source_target_pairs={{0,4},{4,8},{8,12},{12,0},{1,5},{5,9},{9,13},{13,1},{2,6},{6,10},{... | collective-permute-start | bytes 3080 | tf_op jit(solution)/shard_map/ppermute | solution.py:51

commit v3 on v2

--- a/solution.py
+++ b/solution.py
@@ -92,13 +92,14 @@
 
 
 def fetch_kernel(after, x, g, *rest, width):
-    count = (len(rest) - 3) // 2
+    count = (len(rest) - 4) // 2
     sources, outs, own = rest[:count], rest[count : 2 * count], rest[2 * count]
-    own_sem, sem = rest[2 * count + 1 :]
+    own_sem, sem, straight = rest[2 * count + 1 :]
     copies = slice_copies((x, g), lax.axis_index("seq"), width, own, own_sem)
     for j, (src, out) in enumerate(zip(sources, outs)):
-        copies.append(pltpu.make_async_copy(src, out, sem.at[j]))
+        copies.append(pltpu.make_async_copy(src, out if j != 1 else straight, sem.at[j]))
     run_all(copies)
+    outs[1][...] = straight[...].T
 
 
 def feature_kernel(*refs, n, n_tok, block):
@@ -114,7 +115,7 @@
             rows[j, pl.ds(at, n_tok), :] = toks[k][j]
     first = jnp.dot(rows[0], w_in[...], preferred_element_type=jnp.float32)
     outT = lax.dot_general(
-        w_out[...], rows[1], (((0,), (1,)), ((), ())), preferred_element_type=jnp.float32
+        w_out[...], rows[1], (((1,), (1,)), ((), ())), preferred_element_type=jnp.float32
     )
     turned = refs[2 * n + 3]
     for c in range(total // LANES):
@@ -213,9 +214,9 @@
     held = (input_proj, grad_proj, train_store)
     input_proj, grad_proj, train_store, own = call(
         functools.partial(fetch_kernel, width=part),
-        [(a.shape, a.dtype) for a in held] + [slices],
+        [(a.shape if a is not grad_proj else a.shape[::-1], a.dtype) for a in held] + [slices],
         [VMEM] + [HBM] * 5,
-        [pltpu.SemaphoreType.DMA((2,)), pltpu.SemaphoreType.DMA((3,))],
+        [pltpu.SemaphoreType.DMA((2,)), pltpu.SemaphoreType.DMA((3,)), pltpu.VMEM(grad_proj.shape, grad_proj.dtype)],
     )(packed[0], *tokens_in, *map(in_place, held))
     tokens = [own] + exchange(packed, "seq", n, "tokens")
 

time: 41.2 us -> 41.2 us (level)
  no operation moved by 1% of the time
where the time goes in v3:
time: 41.2 us; the launch traced here: 41.1 us
  starting transfers between devices  17.8 us (43%)
  waiting for transfers between devices  16.4 us (40%)
  Pallas kernels  5.55 us (13%)
  between operations  0.7 us (2%)
  other arithmetic  0.57 us (1%)
    ppermute x12, starting transfers between devices, exchange(): got.append(lax.ppermute(arrays[i], axis, list(enumerate(route))))  17.8 us
    ppermute x12, waiting for transfers between devices, exchange(): got.append(lax.ppermute(arrays[i], axis, list(enumerate(route))))  16.4 us
    pallas_call x1, Pallas kernels, body(): call(functools.partial(fetch_kernel, width=part), [(a.shape if a is not g...  2.52 us
    pallas_call x3, Pallas kernels, body(): call(functools.partial(early_kernel, count=len(group), block=block, step=...  1.12 us
    pallas_call x1, Pallas kernels, body(): call(functools.partial(pack_kernel, n=n, width=part), [slices] * (n - 1),...  1.05 us
  transfers between devices with their start and end apart: 12, of which 9 were waited for; matrix products, arithmetic and copies ran while one was open for 0% of the time, Pallas kernels for 9%

profile of v3, /device:TPU:0, one launch (start us, length us, event | category | flops | bytes accessed | tf_op | source)
XLA Modules:
  0.0 41.1 jit_solution(9419297594694476320)
XLA Ops:
  0.0 1.1 %shard_map.64 = (bf16[2,32,1024]{2,1,0:T(8,128)(2,1)S(1)}, bf16[2,32,1024]{2,1,0:T(8,128)(2,1)S(1)}, bf16[2,32,1024]{2,1,0:T(8,128)(2,1)S(1)}) custom-call(bf16[1,32,4096]{2,1,0:T(8,128)(2,1)} %x.3, bf16[1,32,4096]{2,1,0:T(8,128)(2,1)} %g.3), custom_call_target="tpu_custom_call" | custom-call | tf_op jit(solution)/shard_map/pallas_call | solution.py:208
  1.1 5.1 %collective-permute-start = (bf16[2,32,1024]{2,1,0:T(8,128)(2,1)S(1)}, bf16[2,32,1024]{2,1,0:T(8,128)(2,1)S(1)}, u32[]{:S(2)}, u32[]{:S(2)}) collective-permute-start(bf16[2,32,1024]{2,1,0:T(8,128)(2,1)S(1)} %get-tuple-element.20.after), channel_id=1, source_target_pairs={{0,12},{4,8},{8,0},{12,4},{1,13},{5,9},{9,1},{13,5},{2,14},{6,10},... | collective-permute-start | bytes 393224 | tf_op jit(solution)/shard_map/ppermute | solution.py:51
  6.2 0.0 collective-permute-start.1
  6.2 0.9 %collective-permute-start.2 = (bf16[2,32,1024]{2,1,0:T(8,128)(2,1)S(1)}, bf16[2,32,1024]{2,1,0:T(8,128)(2,1)S(1)}, u32[]{:S(2)}, u32[]{:S(2)}) collective-permute-start(bf16[2,32,1024]{2,1,0:T(8,128)(2,1)S(1)} %get-tuple-element.23), channel_id=1, source_target_pairs={{0,4},{4,0},{8,12},{12,8},{1,5},{5,1},{9,13},{13,9},{2,6},{6,2},{1... | collective-permute-start | bytes 393224 | tf_op jit(solution)/shard_map/ppermute | solution.py:51
  7.1 2.5 %shard_map.65 = (bf16[1024,128]{1,0:T(8,128)(2,1)S(1)}, bf16[128,1024]{1,0:T(8,128)(2,1)S(1)}, f32[256,4096]{1,0:T(8,128)S(1)}, bf16[2,32,1024]{2,1,0:T(8,128)(2,1)S(1)}) custom-call(bf16[2,32,1024]{2,1,0:T(8,128)(2,1)S(1)} %get-tuple-element.20.after, bf16[1,32,4096]{2,1,0:T(8,128)(2,1)} %x.3, bf16[1,32,4096]{2,1,0:T(8,128)(2,1)} %g.3, ...), custom_call_target="tpu_custom_call" | custom-call | tf_op jit(solution)/shard_map/pallas_call | solution.py:215
  9.6 5.6 %collective-permute-done.refs_1_ = bf16[2,32,1024]{2,1,0:T(8,128)(2,1)S(1)} collective-permute-done((bf16[2,32,1024]{2,1,0:T(8,128)(2,1)S(1)}, bf16[2,32,1024]{2,1,0:T(8,128)(2,1)S(1)}, u32[]{:S(2)}, u32[]{:S(2)}) %collective-permute-start) | collective-permute-done | bytes 131104 | tf_op jit(solution)/shard_map/ppermute | solution.py:51
  15.2 0.0 collective-permute-done.1.refs_2_
  15.2 0.4 %collective-permute-done.2.refs_3_ = bf16[2,32,1024]{2,1,0:T(8,128)(2,1)S(1)} collective-permute-done((bf16[2,32,1024]{2,1,0:T(8,128)(2,1)S(1)}, bf16[2,32,1024]{2,1,0:T(8,128)(2,1)S(1)}, u32[]{:S(2)}, u32[]{:S(2)}) %collective-permute-start.2) | collective-permute-done | bytes 131104 | tf_op jit(solution)/shard_map/ppermute | solution.py:51
  15.6 0.3 shard_map.66
  15.9 1.6 %collective-permute-start.3 = (f32[160,128]{1,0:T(8,128)S(1)}, f32[160,128]{1,0:T(8,128)S(1)}, u32[]{:S(2)}, u32[]{:S(2)}) collective-permute-start(f32[160,128]{1,0:T(8,128)S(1)} %get-tuple-element.27), channel_id=1, source_target_pairs={{0,8},{4,12},{8,0},{12,4},{1,9},{5,13},{9,1},{13,5},{2,10},{6,14},... | collective-permute-start | bytes 245768 | tf_op jit(solution)/shard_map/ppermute | solution.py:51
  17.6 3.1 %collective-permute-start.4 = (f32[160,128]{1,0:T(8,128)S(1)}, f32[160,128]{1,0:T(8,128)S(1)}, u32[]{:S(2)}, u32[]{:S(2)}) collective-permute-start(f32[160,128]{1,0:T(8,128)S(1)} %get-tuple-element.28), channel_id=1, source_target_pairs={{0,4},{4,8},{8,12},{12,0},{1,5},{5,9},{9,13},{13,1},{2,6},{6,10},{... | collective-permute-start | bytes 245768 | tf_op jit(solution)/shard_map/ppermute | solution.py:51
  20.7 0.7 %collective-permute-start.5 = (f32[160,128]{1,0:T(8,128)S(1)}, f32[160,128]{1,0:T(8,128)S(1)}, u32[]{:S(2)}, u32[]{:S(2)}) collective-permute-start(f32[160,128]{1,0:T(8,128)S(1)} %get-tuple-element.29), channel_id=1, source_target_pairs={{0,12},{4,0},{8,4},{12,8},{1,13},{5,1},{9,5},{13,9},{2,14},{6,2},{... | collective-permute-start | bytes 245768 | tf_op jit(solution)/shard_map/ppermute | solution.py:51
  22.0 3.4 %collective-permute-done.3.refs_1_ = f32[160,128]{1,0:T(8,128)S(1)} collective-permute-done((f32[160,128]{1,0:T(8,128)S(1)}, f32[160,128]{1,0:T(8,128)S(1)}, u32[]{:S(2)}, u32[]{:S(2)}) %collective-permute-start.3) | collective-permute-done | bytes 81952 | tf_op jit(solution)/shard_map/ppermute | solution.py:51
  25.5 0.5 %collective-permute-done.5.refs_3_ = f32[160,128]{1,0:T(8,128)S(1)} collective-permute-done((f32[160,128]{1,0:T(8,128)S(1)}, f32[160,128]{1,0:T(8,128)S(1)}, u32[]{:S(2)}, u32[]{:S(2)}) %collective-permute-start.5) | collective-permute-done | bytes 81952 | tf_op jit(solution)/shard_map/ppermute | solution.py:51
  26.0 0.2 shard_map.67.refs_0_
  26.1 0.0 collective-permute-start.6
  26.1 1.4 %collective-permute-start.7 = (f32[32,128]{1,0:T(8,128)S(1)}, f32[32,128]{1,0:T(8,128)S(1)}, u32[]{:S(2)}, u32[]{:S(2)}) collective-permute-start(f32[32,128]{1,0:T(8,128)S(1)} %shard_map.67.refs_0_), channel_id=1, source_target_pairs={{0,3},{1,2},{2,1},{3,0},{4,7},{5,6},{6,5},{7,4},{8,11},{9,10},{10,... | collective-permute-start | bytes 49160 | tf_op jit(solution)/shard_map/ppermute | solution.py:51
  27.5 0.8 %collective-permute-start.8 = (f32[32,128]{1,0:T(8,128)S(1)}, f32[32,128]{1,0:T(8,128)S(1)}, u32[]{:S(2)}, u32[]{:S(2)}) collective-permute-start(f32[32,128]{1,0:T(8,128)S(1)} %shard_map.67.refs_0_), channel_id=1, source_target_pairs={{0,2},{1,3},{2,0},{3,1},{4,6},{5,7},{6,4},{7,5},{8,10},{9,11},{10,... | collective-permute-start | bytes 49160 | tf_op jit(solution)/shard_map/ppermute | solution.py:51
  28.3 0.4 shard_map.68.refs_1_.refs_0_
  28.7 0.0 collective-permute-done.6.refs_0_
  28.7 0.4 shard_map.69.refs_2_.refs_1_
  29.0 0.3 collective-permute-done.7.refs_0_
  29.3 0.4 shard_map.70.refs_2_
  29.7 1.6 %collective-permute-done.8.refs_3_ = f32[32,128]{1,0:T(8,128)S(1)} collective-permute-done((f32[32,128]{1,0:T(8,128)S(1)}, f32[32,128]{1,0:T(8,128)S(1)}, u32[]{:S(2)}, u32[]{:S(2)}) %collective-permute-start.8) | collective-permute-done | bytes 16416 | tf_op jit(solution)/shard_map/ppermute | solution.py:51
  31.3 0.4 shard_map.71
  31.6 2.2 %collective-permute-start.10 = (f32[1,256]{1,0:T(1,128)S(1)}, f32[1,256]{1,0:T(1,128)S(1)}, u32[]{:S(2)}, u32[]{:S(2)}) collective-permute-start(f32[1,256]{1,0:T(1,128)S(1)} %get-tuple-element.33), channel_id=1, source_target_pairs={{0,8},{4,12},{8,0},{12,4},{1,9},{5,13},{9,1},{13,5},{2,10},{6,14},... | collective-permute-start | bytes 3080 | tf_op jit(solution)/shard_map/ppermute | solution.py:51
  33.8 1.3 %collective-permute-start.11 = (f32[1,256]{1,0:T(1,128)S(1)}, f32[1,256]{1,0:T(1,128)S(1)}, u32[]{:S(2)}, u32[]{:S(2)}) collective-permute-start(f32[1,256]{1,0:T(1,128)S(1)} %get-tuple-element.34), channel_id=1, source_target_pairs={{0,12},{4,0},{8,4},{12,8},{1,13},{5,1},{9,5},{13,9},{2,14},{6,2},{... | collective-permute-start | bytes 3080 | tf_op jit(solution)/shard_map/ppermute | solution.py:51
  35.1 0.7 %collective-permute-start.9 = (f32[1,256]{1,0:T(1,128)S(1)}, f32[1,256]{1,0:T(1,128)S(1)}, u32[]{:S(2)}, u32[]{:S(2)}) collective-permute-start(f32[1,256]{1,0:T(1,128)S(1)} %get-tuple-element.32), channel_id=1, source_target_pairs={{0,4},{4,8},{8,12},{12,0},{1,5},{5,9},{9,13},{13,1},{2,6},{6,10},{... | collective-permute-start | bytes 3080 | tf_op jit(solution)/shard_map/ppermute | solution.py:51
  35.8 0.3 collective-permute-done.10
  36.2 1.2 %collective-permute-done.11 = f32[1,256]{1,0:T(1,128)S(1)} collective-permute-done((f32[1,256]{1,0:T(1,128)S(1)}, f32[1,256]{1,0:T(1,128)S(1)}, u32[]{:S(2)}, u32[]{:S(2)}) %collective-permute-start.11) | collective-permute-done | bytes 1056 | tf_op jit(solution)/shard_map/ppermute | solution.py:51
  37.4 3.1 %collective-permute-done.9 = f32[1,256]{1,0:T(1,128)S(1)} collective-permute-done((f32[1,256]{1,0:T(1,128)S(1)}, f32[1,256]{1,0:T(1,128)S(1)}, u32[]{:S(2)}, u32[]{:S(2)}) %collective-permute-start.9) | collective-permute-done | bytes 1056 | tf_op jit(solution)/shard_map/ppermute | solution.py:51
  40.5 0.6 %add_add_fusion = f32[1,256]{1,0:T(1,128)} fusion(f32[1,256]{1,0:T(1,128)S(1)} %collective-permute-done.11, f32[1,256]{1,0:T(1,128)S(1)} %collective-permute-done.10, f32[1,256]{1,0:T(1,128)S(1)} %get-tuple-element.31, f32[1,256]{1,0:T(1,128)S(1)} %collective-permute-done.9), kind=kLoop, calls=%fused_computation | loop fusion | flops 768 | bytes 5120 | tf_op jit(solution)/shard_map/add | solution.py:258
  (1 shorter events, 0.0 us)
Async XLA Ops:
  1.1 14.1 %collective-permute-start = (bf16[2,32,1024]{2,1,0:T(8,128)(2,1)S(1)}, bf16[2,32,1024]{2,1,0:T(8,128)(2,1)S(1)}, u32[]{:S(2)}, u32[]{:S(2)}) collective-permute-start(bf16[2,32,1024]{2,1,0:T(8,128)(2,1)S(1)} %get-tuple-element.20.after), channel_id=1, source_target_pairs={{0,12},{4,8},{8,0},{12,4},{1,13},{5,9},{9,1},{13,5},{2,14},{6,10},... | collective-permute-start | bytes 393224 | tf_op jit(solution)/shard_map/ppermute | solution.py:51
  6.2 9.0 %collective-permute-start.1 = (bf16[2,32,1024]{2,1,0:T(8,128)(2,1)S(1)}, bf16[2,32,1024]{2,1,0:T(8,128)(2,1)S(1)}, u32[]{:S(2)}, u32[]{:S(2)}) collective-permute-start(bf16[2,32,1024]{2,1,0:T(8,128)(2,1)S(1)} %get-tuple-element.22), channel_id=1, source_target_pairs={{0,8},{4,12},{8,4},{12,0},{1,9},{5,13},{9,5},{13,1},{2,10},{6,14},... | collective-permute-start | bytes 393224 | tf_op jit(solution)/shard_map/ppermute | solution.py:51
  6.2 9.4 %collective-permute-start.2 = (bf16[2,32,1024]{2,1,0:T(8,128)(2,1)S(1)}, bf16[2,32,1024]{2,1,0:T(8,128)(2,1)S(1)}, u32[]{:S(2)}, u32[]{:S(2)}) collective-permute-start(bf16[2,32,1024]{2,1,0:T(8,128)(2,1)S(1)} %get-tuple-element.23), channel_id=1, source_target_pairs={{0,4},{4,0},{8,12},{12,8},{1,5},{5,1},{9,13},{13,9},{2,6},{6,2},{1... | collective-permute-start | bytes 393224 | tf_op jit(solution)/shard_map/ppermute | solution.py:51
  15.9 9.5 %collective-permute-start.3 = (f32[160,128]{1,0:T(8,128)S(1)}, f32[160,128]{1,0:T(8,128)S(1)}, u32[]{:S(2)}, u32[]{:S(2)}) collective-permute-start(f32[160,128]{1,0:T(8,128)S(1)} %get-tuple-element.27), channel_id=1, source_target_pairs={{0,8},{4,12},{8,0},{12,4},{1,9},{5,13},{9,1},{13,5},{2,10},{6,14},... | collective-permute-start | bytes 245768 | tf_op jit(solution)/shard_map/ppermute | solution.py:51
  17.6 7.9 %collective-permute-start.4 = (f32[160,128]{1,0:T(8,128)S(1)}, f32[160,128]{1,0:T(8,128)S(1)}, u32[]{:S(2)}, u32[]{:S(2)}) collective-permute-start(f32[160,128]{1,0:T(8,128)S(1)} %get-tuple-element.28), channel_id=1, source_target_pairs={{0,4},{4,8},{8,12},{12,0},{1,5},{5,9},{9,13},{13,1},{2,6},{6,10},{... | collective-permute-start | bytes 245768 | tf_op jit(solution)/shard_map/ppermute | solution.py:51
  20.7 5.3 %collective-permute-start.5 = (f32[160,128]{1,0:T(8,128)S(1)}, f32[160,128]{1,0:T(8,128)S(1)}, u32[]{:S(2)}, u32[]{:S(2)}) collective-permute-start(f32[160,128]{1,0:T(8,128)S(1)} %get-tuple-element.29), channel_id=1, source_target_pairs={{0,12},{4,0},{8,4},{12,8},{1,13},{5,1},{9,5},{13,9},{2,14},{6,2},{... | collective-permute-start | bytes 245768 | tf_op jit(solution)/shard_map/ppermute | solution.py:51
  26.1 2.5 %collective-permute-start.6 = (f32[32,128]{1,0:T(8,128)S(1)}, f32[32,128]{1,0:T(8,128)S(1)}, u32[]{:S(2)}, u32[]{:S(2)}) collective-permute-start(f32[32,128]{1,0:T(8,128)S(1)} %shard_map.67.refs_0_), channel_id=1, source_target_pairs={{0,1},{1,0},{2,3},{3,2},{4,5},{5,4},{6,7},{7,6},{8,9},{9,8},{10,11... | collective-permute-start | bytes 49160 | tf_op jit(solution)/shard_map/ppermute | solution.py:51
  26.1 3.2 %collective-permute-start.7 = (f32[32,128]{1,0:T(8,128)S(1)}, f32[32,128]{1,0:T(8,128)S(1)}, u32[]{:S(2)}, u32[]{:S(2)}) collective-permute-start(f32[32,128]{1,0:T(8,128)S(1)} %shard_map.67.refs_0_), channel_id=1, source_target_pairs={{0,3},{1,2},{2,1},{3,0},{4,7},{5,6},{6,5},{7,4},{8,11},{9,10},{10,... | collective-permute-start | bytes 49160 | tf_op jit(solution)/shard_map/ppermute | solution.py:51
  27.5 3.7 %collective-permute-start.8 = (f32[32,128]{1,0:T(8,128)S(1)}, f32[32,128]{1,0:T(8,128)S(1)}, u32[]{:S(2)}, u32[]{:S(2)}) collective-permute-start(f32[32,128]{1,0:T(8,128)S(1)} %shard_map.67.refs_0_), channel_id=1, source_target_pairs={{0,2},{1,3},{2,0},{3,1},{4,6},{5,7},{6,4},{7,5},{8,10},{9,11},{10,... | collective-permute-start | bytes 49160 | tf_op jit(solution)/shard_map/ppermute | solution.py:51
  31.6 4.5 %collective-permute-start.10 = (f32[1,256]{1,0:T(1,128)S(1)}, f32[1,256]{1,0:T(1,128)S(1)}, u32[]{:S(2)}, u32[]{:S(2)}) collective-permute-start(f32[1,256]{1,0:T(1,128)S(1)} %get-tuple-element.33), channel_id=1, source_target_pairs={{0,8},{4,12},{8,0},{12,4},{1,9},{5,13},{9,1},{13,5},{2,10},{6,14},... | collective-permute-start | bytes 3080 | tf_op jit(solution)/shard_map/ppermute | solution.py:51
  33.8 3.6 %collective-permute-start.11 = (f32[1,256]{1,0:T(1,128)S(1)}, f32[1,256]{1,0:T(1,128)S(1)}, u32[]{:S(2)}, u32[]{:S(2)}) collective-permute-start(f32[1,256]{1,0:T(1,128)S(1)} %get-tuple-element.34), channel_id=1, source_target_pairs={{0,12},{4,0},{8,4},{12,8},{1,13},{5,1},{9,5},{13,9},{2,14},{6,2},{... | collective-permute-start | bytes 3080 | tf_op jit(solution)/shard_map/ppermute | solution.py:51
  35.1 5.4 %collective-permute-start.9 = (f32[1,256]{1,0:T(1,128)S(1)}, f32[1,256]{1,0:T(1,128)S(1)}, u32[]{:S(2)}, u32[]{:S(2)}) collective-permute-start(f32[1,256]{1,0:T(1,128)S(1)} %get-tuple-element.32), channel_id=1, source_target_pairs={{0,4},{4,8},{8,12},{12,0},{1,5},{5,9},{9,13},{13,1},{2,6},{6,10},{... | collective-permute-start | bytes 3080 | tf_op jit(solution)/shard_map/ppermute | solution.py:51
